TPU v7x, 32 devices: a whole 2x2x4 slice. The times are simulated.
32 devices in a mesh: sx: 2 (over y), sy: 4 (over x, core), net: 4 (over z).
Axes of the slice: x: 2, y: 2, z: 4, core: 2. Of those that a mesh axis runs over, the one named last changes fastest.
Arguments:
- cell_x: int32 [4096, 128], P(('sx', 'sy', 'net')), may hold values from 0 to 14
- cell_y: int32 [4096, 128], P(('sx', 'sy', 'net')), may hold values from 0 to 510
- frac: float32 [2, 4096, 128], P(None, ('sx', 'sy', 'net')), may hold values from 0 to 1
- power: float32 [4096, 128], P(('sx', 'sy', 'net')), may hold values from 0.1 to 1
- block_tile: int32 [4096], P(('sx', 'sy', 'net')), may hold values from 0 to 15
- conductivity: float32 [4, 128, 2048], P(None, 'sx', 'sy'), may hold values from 0.5 to 4
- sink: float32 [128, 2048], P('sx', 'sy'), may hold values from 0.25 to 2
Outputs:
- thermal_state: float32 [4, 128, 2048], P(None, ('sx', 'net'), 'sy')
- instance_locus_derivative: float32 [2, 4096, 128], P(None, ('sx', 'sy', 'net'))
All inputs are finite; a program needn't handle non-finite values.
Results may differ from a plain program's by a relative error of at most 0.0003.
Values sent between devices are 32-bit elements; how exact they have to be, the bound alone decides.
No kernel may reach another device: no remote copies, remote signals or barrier semaphores. Data moves between devices by JAX's collectives and lax.ppermute only.
A program may use at most 64 MiB of HBM per device.

v0:
```python
import jax
import jax.numpy as jnp
from jax import lax
from jax.sharding import PartitionSpec as P

BAND = 16
HEAT_SWEEP_COUNT = 24


def extended(value, sides, width):
    for axis, dim in sides:
        count, length = (lax.axis_size(axis), value.shape[dim])
        up = [(i, (i + 1) % count) for i in range(count - 1)]
        down = [(j, i) for i, j in up]
        last = lax.slice_in_dim(value, length - width, length, axis=dim)
        initial = lax.slice_in_dim(value, 0, width, axis=dim)
        before = lax.ppermute(last, axis, up)
        after = lax.ppermute(initial, axis, down)
        value = jnp.concatenate([before, value, after], axis=dim)
    return value


def harmonic(left_side, right_side):
    return 2.0 * left_side * right_side / (left_side + right_side)


def conductances(conductivity, padded, sink_map):
    x_minus = harmonic(conductivity, padded[:, :-2, 1:-1])
    x_plus = harmonic(conductivity, padded[:, 2:, 1:-1])
    y_minus = harmonic(conductivity, padded[:, 1:-1, :-2])
    y_plus = harmonic(conductivity, padded[:, 1:-1, 2:])
    between = harmonic(conductivity[:-1], conductivity[1:])
    blank = jnp.zeros_like(conductivity[:1])
    z_minus = jnp.concatenate([blank, between], 0)
    z_plus = jnp.concatenate([between, blank], 0)
    outflow = jnp.concatenate([jnp.zeros_like(conductivity[:-1]), sink_map[None]], 0)
    thermal_resistance = 1.0 / (x_minus + x_plus + y_minus + y_plus + z_minus + z_plus + outflow)
    return ((x_minus, x_plus, y_minus, y_plus, z_minus, z_plus), thermal_resistance)


def adjacent_aggregate(field, padded, linkage_quantity):
    x_minus, x_plus, y_minus, y_plus, z_minus, z_plus = linkage_quantity
    blank = jnp.zeros_like(field[:1])
    below = jnp.concatenate([blank, field[:-1]], 0)
    above = jnp.concatenate([field[1:], blank], 0)
    total = x_minus * padded[:, :-2, 1:-1] + x_plus * padded[:, 2:, 1:-1]
    total = total + y_minus * padded[:, 1:-1, :-2] + y_plus * padded[:, 1:-1, 2:]
    return total + z_minus * below + z_plus * above


def full_rim_rows(field):
    return extended(field, (("sx", 1), ("sy", 2)), 1)


def iteration_tally(dissipation_mesh, linkage_quantity, thermal_resistance, rim_of):

    def forward_solve(sweep_index, field):
        return thermal_resistance * (
            dissipation_mesh + adjacent_aggregate(field, rim_of(field), linkage_quantity)
        )

    thermal_state = lax.fori_loop(
        0, HEAT_SWEEP_COUNT - 1, forward_solve, thermal_resistance * dissipation_mesh
    )

    def backward(sweep_index, carry):
        field, total = carry
        field = thermal_resistance * adjacent_aggregate(field, rim_of(field), linkage_quantity)
        return (field, total + field)

    costate_map = thermal_resistance * thermal_state
    costate_aggregate = lax.fori_loop(
        0, HEAT_SWEEP_COUNT - 1, backward, (costate_map, costate_map)
    )[1]
    return (thermal_state, costate_aggregate)


def coefficients(local_column_place, local_line_place, horizontal_part, vertical_part, columns):
    band_pos = lax.broadcasted_iota(jnp.int32, (1, 1, BAND), 2)
    column_pos = lax.broadcasted_iota(jnp.int32, (1, 1, columns), 2)
    floor_bucket_column = (band_pos == local_column_place[..., None]).astype(jnp.float32)
    ceiling_bucket_column = (band_pos == local_column_place[..., None] + 1).astype(jnp.float32)
    low_y = (column_pos == local_line_place[..., None]).astype(jnp.float32)
    high_y = (column_pos == local_line_place[..., None] + 1).astype(jnp.float32)
    horizontal_flux = (1.0 - horizontal_part)[..., None] * floor_bucket_column + horizontal_part[
        ..., None
    ] * ceiling_bucket_column
    vertical_flux = (1.0 - vertical_part)[..., None] * low_y + vertical_part[..., None] * high_y
    return (
        horizontal_flux,
        ceiling_bucket_column - floor_bucket_column,
        vertical_flux,
        high_y - low_y,
    )


def on_device(cell_x, cell_y, frac, power, block_tile, conductivity, sink):
    blocks, width = cell_x.shape
    tiers, rows_tile, columns = conductivity.shape
    tiles = tiers * (rows_tile // BAND)
    group = 4
    turns = blocks // group
    items = (
        cell_x.reshape(turns, group, width),
        cell_y.reshape(turns, group, width),
        frac[0].reshape(turns, group, width),
        frac[1].reshape(turns, group, width),
        power.reshape(turns, group, width),
        block_tile.reshape(turns, group),
    )

    def spread_turn(total, element_amount):
        (
            local_column_place,
            local_line_place,
            horizontal_part,
            vertical_part,
            instance_dissipation,
            patch_ordinals,
        ) = element_amount
        horizontal_flux, horizontal_steepness, vertical_flux, vertical_steepness = coefficients(
            local_column_place, local_line_place, horizontal_part, vertical_part, columns
        )
        block_maps = jnp.einsum(
            "yjh,yjf->yhf",
            instance_dissipation[..., None] * horizontal_flux,
            vertical_flux,
            precision=lax.Precision.HIGHEST,
        )
        member = (patch_ordinals[:, None] == lax.broadcasted_iota(jnp.int32, (1, tiles), 1)).astype(
            jnp.float32
        )
        return (
            total + jnp.einsum("gt,gab->tab", member, block_maps, precision=lax.Precision.HIGHEST),
            None,
        )

    partial_map = lax.scan(spread_turn, jnp.zeros((tiles, BAND, columns), jnp.float32), items)[0]
    partial_map = partial_map.reshape(tiers, rows_tile, columns)
    instance_portion = rows_tile // lax.axis_size("net")
    initial_shift = lax.axis_index("net") * instance_portion
    dissipation_mesh = lax.psum(partial_map, "net")
    linkage_quantity, thermal_resistance = conductances(
        conductivity, full_rim_rows(conductivity), sink
    )
    thermal_state, costate_piece = iteration_tally(
        dissipation_mesh, linkage_quantity, thermal_resistance, full_rim_rows
    )
    thermal_state = lax.dynamic_slice_in_dim(thermal_state, initial_shift, instance_portion, 1)
    adjoint_tiles = costate_piece.reshape(tiles, BAND, columns)

    def gradient_turn(carry, element_amount):
        (
            local_column_place,
            local_line_place,
            horizontal_part,
            vertical_part,
            instance_dissipation,
            patch_ordinals,
        ) = element_amount
        horizontal_flux, horizontal_steepness, vertical_flux, vertical_steepness = coefficients(
            local_column_place, local_line_place, horizontal_part, vertical_part, columns
        )
        local_maps = jnp.take(adjoint_tiles, patch_ordinals, axis=0)
        stacked = jnp.stack([vertical_flux, vertical_steepness])
        factor_multiples = jnp.einsum(
            "kgcb,gab->kgca", stacked, local_maps, precision=lax.Precision.HIGHEST
        )
        horizontal_derivative = instance_dissipation * jnp.sum(
            horizontal_steepness * factor_multiples[0], -1
        )
        vertical_derivative = instance_dissipation * jnp.sum(
            horizontal_flux * factor_multiples[1], -1
        )
        return (carry, jnp.stack([horizontal_derivative, vertical_derivative]))

    grads = lax.scan(gradient_turn, 0.0, items)[1]
    instance_locus_derivative = jnp.moveaxis(grads, 1, 0).reshape(2, blocks, width)
    return (thermal_state, instance_locus_derivative)


def solution(mesh):
    return jax.shard_map(
        on_device,
        mesh=mesh,
        in_specs=(
            P(("sx", "sy", "net"), None),
            P(("sx", "sy", "net"), None),
            P(None, ("sx", "sy", "net"), None),
            P(("sx", "sy", "net"), None),
            P(("sx", "sy", "net")),
            P(None, "sx", "sy"),
            P("sx", "sy"),
        ),
        out_specs=(P(None, ("sx", "net"), "sy"), P(None, ("sx", "sy", "net"), None)),
        check_vma=False,
    )
```

profile of v0, /device:TPU:6, one launch (start us, length us, event | category | flops | bytes accessed | tf_op | source)
XLA Modules:
  0.0 1407.1 jit_solution(3632639459843635625)
XLA Ops:
  8.9 124.2 %while.46 = (s32[]{:T(128)}, f32[16,16,512]{2,0,1:T(8,128)S(1)}, s32[32,4]{1,0:T(8,128)S(1)}, f32[32,4,128]{2,1,0:T(4,128)}, s32[32,4,128]{2,1,0:T(4,128)}, /*in...) while((s32[]{:T(128)}, f32[16,16,512]{2,0,1:T(8,128)S(1)}, ...), condition=%wide.region_1.2_spmd.clone, body=%wide.region_0.1_spmd.clone.sunk | while | flops 58247232 | bytes 1358007 | solution.py:138
  135.6 4.5 collective-permute-start.9
  150.0 24.0 %all-reduce.9.cloned.1.call-done = f32[4,64,512]{2,1,0:T(8,128)} async-done(((f32[4,64,512]{2,1,0:T(8,128)}), f32[4,64,512]{2,1,0:T(8,128)}) %all-reduce.9.cloned.1.call-update) | async-done | bytes 524304 | tf_op jit(solution)/shard_map/psum | solution.py:142
  177.1 480.9 %while.43 = (s32[]{:T(128)}, f32[4,64,512]{2,1,0:T(8,128)}, f32[4,64,512]{2,1,0:T(8,128)S(1)}, f32[4,64,512]{2,1,0:T(8,128)S(1)}, f32[4,64,512]{2,1,0:T(8,128)S(...) while((s32[]{:T(128)}, f32[4,64,512]{2,1,0:T(8,128)}, ...), condition=%wide.region_4.5_spmd, body=%wide.region_3.4_spmd.sunk | while | flops 2753570 | bytes 9319053 | solution.py:62
  181.9 4.2 collective-permute-done.1
  202.8 4.2 collective-permute-done.1
  223.7 4.2 collective-permute-done.1
  244.6 4.2 collective-permute-done.1
  265.4 4.2 collective-permute-done.1
  286.3 4.2 collective-permute-done.1
  307.2 4.2 collective-permute-done.1
  328.1 4.2 collective-permute-done.1
  348.9 4.2 collective-permute-done.1
  369.8 4.2 collective-permute-done.1
  390.7 4.2 collective-permute-done.1
  411.6 4.2 collective-permute-done.1
  495.0 4.2 collective-permute-done.1
  515.9 4.2 collective-permute-done.1
  661.6 483.7 %while.44 = (s32[]{:T(128)}, f32[4,64,512]{2,1,0:T(8,128)}, f32[4,64,512]{2,1,0:T(8,128)}, f32[4,64,512]{2,1,0:T(8,128)S(1)}, f32[4,64,512]{2,1,0:T(8,128)S(1)},...) while((s32[]{:T(128)}, f32[4,64,512]{2,1,0:T(8,128)}, ...), condition=%wide.region_6.7_spmd, body=%wide.region_5.6_spmd.sunk | while | flops 2753570 | bytes 9843341 | solution.py:72
  686.7 4.2 collective-permute-done.5
  749.8 4.2 collective-permute-done.5
  918.1 4.2 collective-permute-done.5
  1086.3 4.2 collective-permute-done.5
  1145.3 253.3 %while.45 = (s32[]{:T(128)}, f32[32,2,4,128]{3,2,1,0:T(4,128)}, f32[32,4,128]{2,1,0:T(4,128)}, s32[32,4,128]{2,1,0:T(4,128)}, s32[32,4]{1,0:T(8,128)}, /*index=5...) while((s32[]{:T(128)}, f32[32,2,4,128]{3,2,1,0:T(4,128)}, ...), condition=%wide.region_10.11_spmd, body=%wide.region_7.10_spmd.sunk | while | flops 103419944 | bytes 4786397 | solution.py:177
  (1161 shorter events, 1284.9 us)
Async XLA Ops:
  7.2 166.9 %all-reduce.9.cloned.1.call-start = ((), (), s32[]{:S(2)}) async-start(), calls=%async_computation | async-start | bytes 1048576 | tf_op jit(solution)/shard_map/psum | solution.py:142
  188.9 6.8 collective-permute-start.3
  209.7 6.8 collective-permute-start.3
  230.6 6.8 collective-permute-start.3
  251.5 6.8 collective-permute-start.3
  272.3 6.8 collective-permute-start.3
  293.2 6.8 collective-permute-start.3
  314.1 6.8 collective-permute-start.3
  335.0 6.8 collective-permute-start.3
  355.8 6.8 collective-permute-start.3
  376.7 6.8 collective-permute-start.3
  397.6 6.8 collective-permute-start.3
  481.1 6.8 collective-permute-start.3
  502.0 6.8 collective-permute-start.3
  522.8 6.8 collective-permute-start.3
  672.6 6.8 collective-permute-start.7
  735.7 6.8 collective-permute-start.7
  798.8 6.8 collective-permute-start.7
  861.9 6.8 collective-permute-start.7
  903.9 6.8 collective-permute-start.7
  967.0 6.8 collective-permute-start.7
  1030.1 6.8 collective-permute-start.7
  1072.2 6.8 collective-permute-start.7
  1135.3 6.8 collective-permute-start.7
  (172 other events, 922.4 us)
Sparse Core Ops, SparseCore 0:
  134.4 39.6 all-reduce.8
where the time goes:
time: 1420 us; the launch traced here: 1410 us
  starting transfers between devices  375 us (26%)
  waiting for transfers between devices  356 us (25%)
  other arithmetic  353 us (25%)
  local copies, waits for them, and re-layouts  168 us (12%)
  matrix products  137 us (10%)
    ppermute x94, waiting for transfers between devices, extended(): before = lax.ppermute(last, axis, up)  328 us
    ppermute x94, starting transfers between devices, extended(): before = lax.ppermute(last, axis, up)  204 us
    ppermute x94, starting transfers between devices, extended(): after = lax.ppermute(initial, axis, down)  171 us
    add x23, other arithmetic, backward(): return (field, total + field)  75.5 us
    mul x23, other arithmetic, forward_solve(): thermal_resistance * (dissipation_mesh + adjacent_aggregate(field, rim_of...  71.9 us
    dot_general x32, matrix products, spread_turn(): jnp.einsum('yjh,yjf->yhf', instance_dissipation[..., None] * horizontal_f...  58.9 us
    dot_general x32, matrix products, gradient_turn(): jnp.einsum('kgcb,gab->kgca', stacked, local_maps, precision=lax.Precision...  58.9 us
    gather x32, local copies, waits for them, and re-layouts, gradient_turn(): local_maps = jnp.take(adjoint_tiles, patch_ordinals, axis=0)  51 us
  transfers between devices with their start and end apart: 189, of which 96 were waited for; matrix products, arithmetic and copies ran while one was open for 3% of the time, Pallas kernels for 0%

commit v1 on v0

v1 whole, which is shorter than its diff:
```python
import functools

import jax
import jax.numpy as jnp
from jax import lax
from jax.experimental import pallas as pl
from jax.experimental.pallas import tpu as pltpu
from jax.sharding import PartitionSpec as P

BAND = 16
HEAT_SWEEP_COUNT = 24
LANES = 128
SUB = 8
HALO_X = 48
HALO_Y = 64
F32 = jnp.float32
BF16 = jnp.bfloat16


def iota(shape, dim):
    return lax.broadcasted_iota(jnp.int32, shape, dim)


def split2(value):
    high = value.astype(BF16)
    return high, (value - high.astype(F32)).astype(BF16)


def spread_kernel(tile_ref, x_ref, y_ref, frac_ref, power_ref, out_ref, acc_ref, *, unroll):
    blocks, width = x_ref.shape
    tiers, rows, columns = out_ref.shape
    bands = rows // BAND
    acc_ref[...] = jnp.zeros_like(acc_ref)

    def one(b):
        x = x_ref[pl.ds(b, 1), :]
        y = y_ref[pl.ds(b, 1), :]
        fx = frac_ref[0, pl.ds(b, 1), :]
        fy = frac_ref[1, pl.ds(b, 1), :]
        p = power_ref[pl.ds(b, 1), :]
        band = iota((BAND, width), 0)
        flux = jnp.where(band == x, p * (1.0 - fx), jnp.where(band == x + 1, p * fx, 0.0))
        low = split2(flux * (1.0 - fy))
        high = split2(flux * fy)
        weights = jnp.concatenate([low[0], low[1], high[0], high[1]], 0)
        onehot = (iota((columns, width), 0) == y).astype(F32).astype(BF16)
        maps = lax.dot_general(weights, onehot, (((1,), (1,)), ((), ())), preferred_element_type=F32)
        return maps[0:BAND] + maps[BAND : 2 * BAND], maps[2 * BAND : 3 * BAND] + maps[3 * BAND :]

    def turn(g, carry):
        for k in range(unroll):
            b = g * unroll + k
            low, high = one(b)
            tile = tile_ref[b]
            acc_ref[tile, 0] += low
            acc_ref[tile, 1] += high
        return carry

    lax.fori_loop(0, blocks // unroll, turn, 0)
    for tile in range(tiers * bands):
        band = tile % bands
        out_ref[tile // bands, band * BAND : (band + 1) * BAND, :] = acc_ref[tile, 0] + pltpu.roll(
            acc_ref[tile, 1], 1, 1
        )


def spread(cell_x, cell_y, frac, power, block_tile, shape):
    blocks, width = cell_x.shape
    tiers, rows, columns = shape
    tiles = tiers * (rows // BAND)
    vmem = pl.BlockSpec(memory_space=pltpu.VMEM)
    return pl.pallas_call(
        functools.partial(spread_kernel, unroll=4),
        out_shape=jax.ShapeDtypeStruct(shape, F32),
        in_specs=[pl.BlockSpec(memory_space=pltpu.SMEM)] + [vmem] * 4,
        out_specs=vmem,
        scratch_shapes=[pltpu.VMEM((tiles, 2, BAND, columns), F32)],
        name="spread",
    )(block_tile, cell_x, cell_y, frac, power)


def gather_kernel(tile_ref, x_ref, y_ref, frac_ref, power_ref, adj_ref, out_ref, maps_ref, *, unroll):
    blocks, width = x_ref.shape
    tiers, rows, columns = adj_ref.shape
    bands = rows // BAND
    for tile in range(tiers * bands):
        band = tile % bands
        field = adj_ref[tile // bands, band * BAND : (band + 1) * BAND, :]
        along_x = pltpu.roll(field, BAND - 1, 0) - field
        along_y = pltpu.roll(field, columns - 1, 1) - field
        mixed = pltpu.roll(along_x, columns - 1, 1) - along_x
        parts = split2(along_x) + split2(along_y) + split2(mixed)
        for n, part in enumerate(parts):
            maps_ref[tile, n * BAND : (n + 1) * BAND, :] = part

    def one(b):
        x = x_ref[pl.ds(b, 1), :]
        y = y_ref[pl.ds(b, 1), :]
        fx = frac_ref[0, pl.ds(b, 1), :]
        fy = frac_ref[1, pl.ds(b, 1), :]
        p = power_ref[pl.ds(b, 1), :]
        onehot = (iota((columns, width), 0) == y).astype(F32).astype(BF16)
        got = lax.dot_general(
            maps_ref[tile_ref[b]], onehot, (((1,), (0,)), ((), ())), preferred_element_type=F32
        )
        along_x = got[0:BAND] + got[BAND : 2 * BAND]
        along_y = got[2 * BAND : 3 * BAND] + got[3 * BAND : 4 * BAND]
        mixed = got[4 * BAND : 5 * BAND] + got[5 * BAND : 6 * BAND]
        here = iota((BAND, width), 0) == x
        by_x = jnp.sum(jnp.where(here, along_x + fy * mixed, 0.0), 0, keepdims=True)
        by_y = jnp.sum(jnp.where(here, along_y + fx * mixed, 0.0), 0, keepdims=True)
        out_ref[0, pl.ds(b, 1), :] = p * by_x
        out_ref[1, pl.ds(b, 1), :] = p * by_y

    def turn(g, carry):
        for k in range(unroll):
            one(g * unroll + k)
        return carry

    lax.fori_loop(0, blocks // unroll, turn, 0)


def gather(cell_x, cell_y, frac, power, block_tile, adjoint):
    tiers, rows, columns = adjoint.shape
    tiles = tiers * (rows // BAND)
    vmem = pl.BlockSpec(memory_space=pltpu.VMEM)
    return pl.pallas_call(
        functools.partial(gather_kernel, unroll=4),
        out_shape=jax.ShapeDtypeStruct(frac.shape, F32),
        in_specs=[pl.BlockSpec(memory_space=pltpu.SMEM)] + [vmem] * 5,
        out_specs=vmem,
        scratch_shapes=[pltpu.VMEM((tiles, 6 * BAND, columns), BF16)],
        name="gather",
    )(block_tile, cell_x, cell_y, frac, power, adjoint)


def next_lane(pair, last):
    a, b = (pltpu.roll(v, LANES - 1, 1) for v in pair)
    return [jnp.where(last, b, a), jnp.where(last, a, b)]


def prev_lane(pair, first):
    a, b = (pltpu.roll(v, 1, 1) for v in pair)
    return [jnp.where(first, b, a), jnp.where(first, a, b)]


def harmonic(left_side, right_side):
    return 2.0 * left_side * right_side / (left_side + right_side)


def coef_kernel(place_ref, cond_ref, bx_ref, by_ref, bz_ref, scale_ref, k_ref, *, tiers, rows, span, grid_x, grid_y):
    steps = bx_ref.shape[2]
    total_rows = steps * SUB
    row0, row_wrap, col0 = place_ref[0], place_ref[1], place_ref[2]
    lane = iota((SUB, LANES), 1)
    first, last = lane == 0, lane == LANES - 1

    def row_at(r):
        r = jnp.where(r >= total_rows, r - total_rows, r)
        return jnp.where(r < row_wrap, row0 + r, row0 + r - total_rows)

    def col_at(c):
        c = jnp.where(c >= 2 * LANES, c - 2 * LANES, c)
        before = c >= 2 * LANES - HALO_Y
        after = c < span + HALO_Y
        return jnp.where(after, col0 + c, jnp.where(before, col0 + c - 2 * LANES, -8))

    def inside(g, size):
        return (g >= 0) & (g < size)

    cols = [col_at(lane + j * LANES) for j in range(2)]
    cols_next = [col_at(lane + j * LANES + 1) for j in range(2)]
    col_ok = [inside(c, grid_y) for c in cols]
    col_link = [a & inside(n, grid_y) & (n == c + 1) for a, c, n in zip(col_ok, cols, cols_next)]
    sub = iota((SUB, LANES), 0) * steps
    row_ok, row_link = [], []
    for i in range(steps):
        r, n = row_at(sub + i), row_at(sub + i + 1)
        row_ok.append(inside(r, grid_x))
        row_link.append(row_ok[-1] & inside(n, grid_x) & (n == r + 1))

    for i in range(steps):
        for j in range(2):
            for t in range(tiers):
                k = cond_ref[t, j, pl.ds(i, SUB, stride=steps), :]
                k_ref[t, j, i] = jnp.where(row_ok[i] & col_ok[j], k, 1.0)
    for i in range(steps):
        for t in range(tiers):
            here = [k_ref[t, j, i] for j in range(2)]
            below = [k_ref[t, j, (i + 1) % steps] for j in range(2)]
            if i == steps - 1:
                below = [pltpu.roll(v, SUB - 1, 0) for v in below]
            beside = next_lane(here, last)
            for j in range(2):
                bx_ref[t, j, i] = jnp.where(row_link[i] & col_ok[j], harmonic(here[j], below[j]), 0.0)
                by_ref[t, j, i] = jnp.where(row_ok[i] & col_link[j], harmonic(here[j], beside[j]), 0.0)
                if t + 1 < tiers:
                    bz_ref[t, j, i] = jnp.where(
                        row_ok[i] & col_ok[j], harmonic(here[j], k_ref[t + 1, j, i]), 0.0
                    )
    for i in range(steps):
        for t in range(tiers):
            back = prev_lane([by_ref[t, j, i] for j in range(2)], first)
            for j in range(2):
                up = bx_ref[t, j, (i - 1) % steps]
                if i == 0:
                    up = pltpu.roll(up, 1, 0)
                out = bx_ref[t, j, i] + up + by_ref[t, j, i] + back[j]
                if t:
                    out = out + bz_ref[t - 1, j, i]
                if t + 1 < tiers:
                    out = out + bz_ref[t, j, i]
                else:
                    out = out + cond_ref[tiers, j, pl.ds(i, SUB, stride=steps), :]
                out = jnp.where(row_ok[i] & col_ok[j], out, 1.0)
                scale = lax.rsqrt(out)
                scale_ref[t, j, i] = scale * (1.5 - 0.5 * out * scale * scale)
    for i in range(steps):
        for t in range(tiers):
            here = [scale_ref[t, j, i] for j in range(2)]
            below = [scale_ref[t, j, (i + 1) % steps] for j in range(2)]
            if i == steps - 1:
                below = [pltpu.roll(v, SUB - 1, 0) for v in below]
            beside = next_lane(here, last)
            for j in range(2):
                bx_ref[t, j, i] = here[j] * bx_ref[t, j, i] * below[j]
                by_ref[t, j, i] = here[j] * by_ref[t, j, i] * beside[j]
                if t + 1 < tiers:
                    bz_ref[t, j, i] = here[j] * bz_ref[t, j, i] * scale_ref[t + 1, j, i]


def coefs(place, cond_window, tiers, rows, span, grid_x, grid_y):
    steps = cond_window.shape[2] // SUB
    shape = (tiers, 2, steps, SUB, LANES)
    vmem = pl.BlockSpec(memory_space=pltpu.VMEM)
    sds = jax.ShapeDtypeStruct(shape, F32)
    return pl.pallas_call(
        functools.partial(
            coef_kernel, tiers=tiers, rows=rows, span=span, grid_x=grid_x, grid_y=grid_y
        ),
        out_shape=(sds, sds, jax.ShapeDtypeStruct((tiers - 1,) + shape[1:], F32), sds),
        in_specs=[pl.BlockSpec(memory_space=pltpu.SMEM), vmem],
        out_specs=(vmem,) * 4,
        scratch_shapes=[pltpu.VMEM(shape, F32)],
        name="coefs",
    )(place, cond_window)


def sweep(u_ref, q_ref, bx_ref, by_ref, bz_ref):
    tiers, _, steps = u_ref.shape[:3]
    lane = iota((SUB, LANES), 1)
    first, last = lane == 0, lane == LANES - 1
    cells = [(t, j) for t in range(tiers) for j in range(2)]
    wrapped = {c: pltpu.roll(u_ref[c[0], c[1], 0], SUB - 1, 0) for c in cells}
    from_up = {
        c: pltpu.roll(bx_ref[c[0], c[1], steps - 1] * u_ref[c[0], c[1], steps - 1], 1, 0) for c in cells
    }
    here = {c: u_ref[c[0], c[1], 0] for c in cells}
    for i in range(steps):
        below = wrapped if i == steps - 1 else {c: u_ref[c[0], c[1], i + 1] for c in cells}
        total = {}
        for c in cells:
            t, j = c
            bx = bx_ref[t, j, i]
            total[c] = (q_ref[t, j, i] + from_up[c]) + bx * below[c]
            from_up[c] = bx * here[c]
        for t in range(tiers):
            pair = [here[t, j] for j in range(2)]
            by = [by_ref[t, j, i] for j in range(2)]
            ahead = next_lane(pair, last)
            back = prev_lane([b * v for b, v in zip(by, pair)], first)
            for j in range(2):
                total[t, j] = total[t, j] + (by[j] * ahead[j] + back[j])
        for t in range(tiers - 1):
            for j in range(2):
                bz = bz_ref[t, j, i]
                total[t, j] = total[t, j] + bz * here[t + 1, j]
                total[t + 1, j] = total[t + 1, j] + bz * here[t, j]
        for c in cells:
            u_ref[c[0], c[1], i] = total[c]
        here = below


def solve_kernel(p_ref, bx_ref, by_ref, bz_ref, scale_ref, temp_ref, adj_ref, u_ref, q_ref, o_ref):
    tiers, _, steps = u_ref.shape[:3]
    rows = temp_ref.shape[1]
    for t in range(tiers):
        for j in range(2):
            for i in range(steps):
                value = scale_ref[t, j, i] * p_ref[t, j, pl.ds(i, SUB, stride=steps), :]
                u_ref[t, j, i] = value
                q_ref[t, j, i] = value

    def step(k, carry):
        sweep(u_ref, q_ref, bx_ref, by_ref, bz_ref)
        return carry

    def emit(dst_ref):
        for t in range(tiers):
            for i in range(steps):
                o_ref[t, pl.ds(i, SUB, stride=steps), :] = scale_ref[t, 0, i] * u_ref[t, 0, i]
            dst_ref[t] = o_ref[t, :rows, :]

    lax.fori_loop(0, HEAT_SWEEP_COUNT - 1, step, 0)
    emit(temp_ref)
    for t in range(tiers):
        for j in range(2):
            for i in range(steps):
                scale = scale_ref[t, j, i]
                value = scale * scale * u_ref[t, j, i]
                u_ref[t, j, i] = value
                q_ref[t, j, i] = value
    lax.fori_loop(0, HEAT_SWEEP_COUNT - 1, step, 0)
    emit(adj_ref)


def solve(p_window, bx, by, bz, scale, rows):
    tiers, _, steps = scale.shape[:3]
    vmem = pl.BlockSpec(memory_space=pltpu.VMEM)
    sds = jax.ShapeDtypeStruct((tiers, rows, LANES), F32)
    return pl.pallas_call(
        solve_kernel,
        out_shape=(sds, sds),
        in_specs=[vmem] * 5,
        out_specs=(vmem,) * 2,
        scratch_shapes=[
            pltpu.VMEM(scale.shape, F32),
            pltpu.VMEM(scale.shape, F32),
            pltpu.VMEM((tiers, steps * SUB, LANES), F32),
        ],
        name="solve",
    )(p_window, bx, by, bz, scale)


def on_device(cell_x, cell_y, frac, power, block_tile, conductivity, sink):
    tiers, rows, columns = conductivity.shape
    n_sx, n_sy, n_net = (lax.axis_size(a) for a in ("sx", "sy", "net"))
    sx, sy, net = (lax.axis_index(a) for a in ("sx", "sy", "net"))
    span = columns // n_net
    turned = sy % 2 == 1
    chunk_id = jnp.where(turned, n_net - 1 - net, net)

    order = [s * n_net + (n_net - 1 - r if s % 2 else r) for s in range(n_sy) for r in range(n_net)]
    to_right = list(zip(order[:-1], order[1:]))
    to_left = [(b, a) for a, b in to_right]

    def window(chunk):
        right = lax.ppermute(chunk[..., :HALO_Y], ("sy", "net"), to_left)
        left = lax.ppermute(chunk[..., span - HALO_Y :], ("sy", "net"), to_right)
        gap = jnp.zeros(chunk.shape[:-1] + (2 * LANES - span - 2 * HALO_Y,), F32)
        strip = jnp.concatenate([chunk, right, gap, left], -1)
        if n_sx == 2:
            edge = lax.dynamic_slice_in_dim(strip, (1 - sx) * (rows - HALO_X), HALO_X, 1)
            parts = [strip, lax.ppermute(edge, "sx", [(0, 1), (1, 0)])]
        else:
            up = [(i, i + 1) for i in range(n_sx - 1)]
            down = [(b, a) for a, b in up]
            after = lax.ppermute(strip[:, :HALO_X], "sx", down)
            before = lax.ppermute(strip[:, rows - HALO_X :], "sx", up)
            parts = [strip, after, before]
        full = jnp.concatenate(parts, 1)
        return jnp.stack([full[..., :LANES], full[..., LANES:]], 1)

    material = jnp.concatenate([conductivity, sink[None]], 0)
    cond_window = window(lax.dynamic_slice_in_dim(material, chunk_id * span, span, 2))
    total_rows = cond_window.shape[2]
    wrap = jnp.where(sx == 0, total_rows, rows) if n_sx == 2 else rows + HALO_X
    place = jnp.stack([sx * rows, wrap, (sy * n_net + chunk_id) * span]).astype(jnp.int32)
    bx, by, bz, scale = coefs(
        place, cond_window, tiers, rows, span, n_sx * rows, n_sy * columns
    )

    partial_map = spread(cell_x, cell_y, frac, power, block_tile, conductivity.shape)

    def chunk_of(value, rank):
        place_of = jnp.where(turned, n_net - 1 - rank, rank)
        return lax.dynamic_slice_in_dim(value, place_of * span, span, 2)

    def ring(distance):
        return [(i, (i + distance) % n_net) for i in range(n_net)]

    own = chunk_of(partial_map, net)
    for d in range(1, n_net):
        own = own + lax.ppermute(chunk_of(partial_map, (net + d) % n_net), "net", ring(d))
    temp, adj = solve(window(own), bx, by, bz, scale, rows)
    temp, adj = temp[..., :span], adj[..., :span]

    share = rows // n_net
    temp_full = jnp.zeros((tiers, share, columns), F32)
    adj_full = jnp.zeros((tiers, rows, columns), F32)
    for d in range(n_net):
        source = (net - d) % n_net
        at = jnp.where(turned, n_net - 1 - source, source) * span
        piece = lax.dynamic_slice_in_dim(temp, (net + d) % n_net * share, share, 1)
        adj_piece = adj
        if d:
            piece = lax.ppermute(piece, "net", ring(d))
            adj_piece = lax.ppermute(adj, "net", ring(d))
        temp_full = lax.dynamic_update_slice_in_dim(temp_full, piece, at, 2)
        adj_full = lax.dynamic_update_slice_in_dim(adj_full, adj_piece, at, 2)
    return temp_full, gather(cell_x, cell_y, frac, power, block_tile, adj_full)


def solution(mesh):
    return jax.shard_map(
        on_device,
        mesh=mesh,
        in_specs=(
            P(("sx", "sy", "net"), None),
            P(("sx", "sy", "net"), None),
            P(None, ("sx", "sy", "net"), None),
            P(("sx", "sy", "net"), None),
            P(("sx", "sy", "net")),
            P(None, "sx", "sy"),
            P("sx", "sy"),
        ),
        out_specs=(P(None, ("sx", "net"), "sy"), P(None, ("sx", "sy", "net"), None)),
        check_vma=False,
    )
```

time: 1420 us -> 102 us (0.07)
  starting transfers between devices: 375 us -> 24.1 us
  other arithmetic: 353 us -> 4.6 us
  waiting for transfers between devices: 356 us -> 23.8 us
  local copies, waits for them, and re-layouts: 168 us -> 3.01 us
  matrix products: 137 us -> 0 us
  Pallas kernels: 0 us -> 43.7 us
    ppermute x188 -> x15, starting transfers between devices: 375 us -> 24.1 us  [the longest x2 7.84 us: window(): left = lax.ppermute(chunk[..., span - HALO_Y:], ('sy', 'net'), to_right)]
    ppermute x188 -> x15, waiting for transfers between devices: 332 us -> 23.8 us  [the longest x3 10.5 us: on_device(): piece = lax.ppermute(piece, 'net', ring(d))]
    dot_general x96 -> x0, matrix products: 137 us -> none  [the longest x32 58.9 us: spread_turn(): jnp.einsum('yjh,yjf->yhf', instance_dissipation[..., None] * horizontal_f...]
    add x119 -> x1, other arithmetic: 132 us -> 0.93 us  [on_device(): own + lax.ppermute(chunk_of(partial_map, (net + d) % n_net), 'net', ring(d))]
    mul x57 -> x0, other arithmetic: 98.1 us -> none  [the longest x23 71.9 us: forward_solve(): thermal_resistance * (dissipation_mesh + adjacent_aggregate(field, rim_of...]
    gather x32 -> x0, local copies, waits for them, and re-layouts: 51 us -> none  [gradient_turn(): local_maps = jnp.take(adjoint_tiles, patch_ordinals, axis=0)]
    while x47 -> x0, local copies, waits for them, and re-layouts: 49 us -> none
    pallas_call x0 -> x4, Pallas kernels: none -> 43.7 us  [the longest x1 16.5 us: solve(): pl.pallas_call(solve_kernel, out_shape=(sds, sds), in_specs=[vmem] * 5, o...]
  transfers between devices with their start and end apart: 189 -> 15, of which waited for: 96 -> 8; matrix products, arithmetic and copies ran while one was open for 3% -> 4% of each run, Pallas kernels for 0% -> 14%
where the time goes in v1:
time: 102 us; the launch traced here: 100 us
  Pallas kernels  43.7 us (43%)
  starting transfers between devices  24.1 us (24%)
  waiting for transfers between devices  23.8 us (23%)
  other arithmetic  4.6 us (5%)
  local copies, waits for them, and re-layouts  3.01 us (3%)
    pallas_call x1, Pallas kernels, solve(): pl.pallas_call(solve_kernel, out_shape=(sds, sds), in_specs=[vmem] * 5, o...  16.5 us
    pallas_call x1, Pallas kernels, gather(): pl.pallas_call(functools.partial(gather_kernel, unroll=4), out_shape=jax....  12.7 us
    pallas_call x1, Pallas kernels, spread(): pl.pallas_call(functools.partial(spread_kernel, unroll=4), out_shape=jax....  11.6 us
    ppermute x3, waiting for transfers between devices, on_device(): piece = lax.ppermute(piece, 'net', ring(d))  10.5 us
    ppermute x3, waiting for transfers between devices, on_device(): lax.ppermute(chunk_of(partial_map, (net + d) % n_net), 'net', ring(d))  9.11 us
    ppermute x2, starting transfers between devices, window(): left = lax.ppermute(chunk[..., span - HALO_Y:], ('sy', 'net'), to_right)  7.84 us
    ppermute x3, starting transfers between devices, on_device(): adj_piece = lax.ppermute(adj, 'net', ring(d))  5.47 us
    ppermute x3, starting transfers between devices, on_device(): lax.ppermute(chunk_of(partial_map, (net + d) % n_net), 'net', ring(d))  4.67 us
  transfers between devices with their start and end apart: 15, of which 8 were waited for; matrix products, arithmetic and copies ran while one was open for 4% of the time, Pallas kernels for 14%

profile of v1, /device:TPU:6, one launch (start us, length us, event | category | flops | bytes accessed | tf_op | source)
XLA Modules:
  0.0 100.2 jit_solution(15354408984222229613)
XLA Ops:
  0.7 0.9 fusion.4
  1.7 1.9 %collective-permute-start.6 = (f32[5,64,64]{2,1,0:T(8,128)S(1)}, f32[5,64,64]{2,1,0:T(8,128)S(1)}, u32[]{:S(2)}, u32[]{:S(2)}) collective-permute-start(f32[5,64,64]{2,1,0:T(8,128)S(1)} %get-tuple-element.22), channel_id=1, source_target_pairs={{1,0},{2,1},{3,2},{7,3},{6,7},{5,6},{4,5},{8,4},{9,8},{10,9},{11,1... | collective-permute-start | bytes 245768 | tf_op jit(solution)/shard_map/ppermute | solution.py:348
  3.6 3.9 %collective-permute-start.7 = (f32[5,64,64]{2,1,0:T(8,128)S(1)}, f32[5,64,64]{2,1,0:T(8,128)S(1)}, u32[]{:S(2)}, u32[]{:S(2)}) collective-permute-start(f32[5,64,64]{2,1,0:T(8,128)S(1)} %get-tuple-element.21), channel_id=1, source_target_pairs={{0,1},{1,2},{2,3},{3,7},{7,6},{6,5},{5,4},{4,8},{8,9},{9,10},{10,1... | collective-permute-start | bytes 245768 | tf_op jit(solution)/shard_map/ppermute | solution.py:349
  7.6 11.6 %spread.1 = f32[4,64,512]{2,1,0:T(8,128)} custom-call(s32[128]{0:T(128)} %tile_ref.3, s32[128,128]{1,0:T(8,128)} %x_ref.3, s32[128,128]{1,0:T(8,128)} %y_ref.3, f32[2,128,128]{2,1,0:T(8,128)} %frac_ref.3, f32[128,128]{1,0:T(8,128)} %power_ref.3), custom_call_target="tpu_custom_call" | custom-call | tf_op jit(solution)/shard_map/spread/pallas_call | solution.py:72
  19.2 1.1 %constant_dynamic-slice_fusion.5 = (f32[4,64,128]{2,1,0:T(8,128)S(1)}, f32[4,64,128]{2,1,0:T(8,128)S(1)}, f32[4,64,128]{2,1,0:T(8,128)S(1)}) fusion(f32[4,64,512]{2,1,0:T(8,128)} %spread.1, s32[]{:T(128)S(6)} %select_n.122, s32[]{:T(128)S(6)} %select_n.128, s32[]{:T(128)S(6)} %select_n.125), kind=kLoop, calls=%fused_computation.35 | loop fusion | bytes 786444 | tf_op jit(solution)/shard_map/dynamic_slice | solution.py:377
  20.3 2.1 %collective-permute-start.2 = (f32[4,64,128]{2,1,0:T(8,128)S(1)}, f32[4,64,128]{2,1,0:T(8,128)S(1)}, u32[]{:S(2)}, u32[]{:S(2)}) collective-permute-start(f32[4,64,128]{2,1,0:T(8,128)S(1)} %get-tuple-element.17), channel_id=1, source_target_pairs={{0,3},{1,0},{2,1},{3,2},{4,7},{5,4},{6,5},{7,6},{8,11},{9,8},{10,9... | collective-permute-start | bytes 393224 | tf_op jit(solution)/shard_map/ppermute | solution.py:384
  22.4 1.0 collective-permute-start.1
  23.4 1.6 %collective-permute-start = (f32[4,64,128]{2,1,0:T(8,128)S(1)}, f32[4,64,128]{2,1,0:T(8,128)S(1)}, u32[]{:S(2)}, u32[]{:S(2)}) collective-permute-start(f32[4,64,128]{2,1,0:T(8,128)S(1)} %get-tuple-element.16), channel_id=1, source_target_pairs={{0,1},{1,2},{2,3},{3,0},{4,5},{5,6},{6,7},{7,4},{8,9},{9,10},{10,1... | collective-permute-start | bytes 393224 | tf_op jit(solution)/shard_map/ppermute | solution.py:384
  26.4 8.3 %collective-permute-done.1 = f32[4,64,128]{2,1,0:T(8,128)S(1)} collective-permute-done((f32[4,64,128]{2,1,0:T(8,128)S(1)}, f32[4,64,128]{2,1,0:T(8,128)S(1)}, u32[]{:S(2)}, u32[]{:S(2)}) %collective-permute-start.1) | collective-permute-done | bytes 131104 | tf_op jit(solution)/shard_map/ppermute | solution.py:384
  34.7 0.9 add_add_fusion
  35.8 1.9 %collective-permute-start.3 = (f32[4,64,64]{2,1,0:T(8,128)S(1)}, f32[4,64,64]{2,1,0:T(8,128)S(1)}, u32[]{:S(2)}, u32[]{:S(2)}) collective-permute-start(f32[4,64,64]{2,1,0:T(8,128)S(1)} %get-tuple-element.28), channel_id=1, source_target_pairs={{1,0},{2,1},{3,2},{7,3},{6,7},{5,6},{4,5},{8,4},{9,8},{10,9},{11,1... | collective-permute-start | bytes 196616 | tf_op jit(solution)/shard_map/ppermute | solution.py:348
  37.7 3.9 %collective-permute-start.4 = (f32[4,64,64]{2,1,0:T(8,128)S(1)}, f32[4,64,64]{2,1,0:T(8,128)S(1)}, u32[]{:S(2)}, u32[]{:S(2)}) collective-permute-start(f32[4,64,64]{2,1,0:T(8,128)S(1)} %get-tuple-element.27), channel_id=1, source_target_pairs={{0,1},{1,2},{2,3},{3,7},{7,6},{6,5},{5,4},{4,8},{8,9},{9,10},{10,1... | collective-permute-start | bytes 196616 | tf_op jit(solution)/shard_map/ppermute | solution.py:349
  42.8 1.4 %collective-permute-done.4 = f32[4,64,64]{2,1,0:T(8,128)S(1)} collective-permute-done((f32[4,64,64]{2,1,0:T(8,128)S(1)}, f32[4,64,64]{2,1,0:T(8,128)S(1)}, u32[]{:S(2)}, u32[]{:S(2)}) %collective-permute-start.4) | collective-permute-done | bytes 65568 | tf_op jit(solution)/shard_map/ppermute | solution.py:349
  45.0 0.9 pad_maximum_fusion.1.cond_ref
  45.8 2.9 %coefs.1 = (f32[4,2,14,8,128]{4,3,2,1,0:T(8,128)}, f32[4,2,14,8,128]{4,3,2,1,0:T(8,128)}, f32[3,2,14,8,128]{4,3,2,1,0:T(8,128)}, f32[4,2,14,8,128]{4,3,2,1,0:T(8,128)}) custom-call(s32[3]{0:T(128)} %pad_add_fusion.place_ref, f32[5,2,112,128]{3,2,1,0:T(8,128)} %pad_maximum_fusion.1.cond_ref), custom_call_target="tpu_custom_call" | custom-call | tf_op jit(solution)/shard_map/coefs/pallas_call | solution.py:237
  48.7 2.4 %collective-permute-done.5 = f32[4,48,256]{2,1,0:T(8,128)S(1)} collective-permute-done((f32[4,48,256]{2,1,0:T(8,128)S(1)}, f32[4,48,256]{2,1,0:T(8,128)S(1)}, u32[]{:S(2)}, u32[]{:S(2)}) %collective-permute-start.5) | collective-permute-done | bytes 196640 | tf_op jit(solution)/shard_map/ppermute | solution.py:354
  51.2 0.8 pad_maximum_fusion.3.p_ref
  52.0 16.5 %solve.1 = (f32[4,64,128]{2,1,0:T(8,128)}, f32[4,64,128]{2,1,0:T(8,128)}) custom-call(f32[4,2,112,128]{3,2,1,0:T(8,128)} %pad_maximum_fusion.3.p_ref, f32[4,2,14,8,128]{4,3,2,1,0:T(8,128)} %get-tuple-element.8.bx_ref, f32[4,2,14,8,128]{4,3,2,1,0:T(8,128)} %get-tuple-element.9.by_ref, f32[3,2,14,8,128]{4,3,2,1,0:T(8,128)} %get-tuple-element.10.bz_ref, ...), custom_call_target="tpu_custom_call" | custom-call | tf_op jit(solution)/shard_map/solve/pallas_call | solution.py:321
  68.5 1.6 %collective-permute-start.12 = (f32[4,64,128]{2,1,0:T(8,128)}, f32[4,64,128]{2,1,0:T(8,128)S(1)}, u32[]{:S(2)}, u32[]{:S(2)}) collective-permute-start(f32[4,64,128]{2,1,0:T(8,128)} %get-tuple-element.13), channel_id=1, source_target_pairs={{0,1},{1,2},{2,3},{3,0},{4,5},{5,6},{6,7},{7,4},{8,9},{9,10},{10,1... | collective-permute-start | bytes 393224 | tf_op jit(solution)/shard_map/ppermute | solution.py:398
  70.2 2.2 %collective-permute-start.13 = (f32[4,64,128]{2,1,0:T(8,128)}, f32[4,64,128]{2,1,0:T(8,128)S(1)}, u32[]{:S(2)}, u32[]{:S(2)}) collective-permute-start(f32[4,64,128]{2,1,0:T(8,128)} %get-tuple-element.13), channel_id=1, source_target_pairs={{0,2},{1,3},{2,0},{3,1},{4,6},{5,7},{6,4},{7,5},{8,10},{9,11},{10,... | collective-permute-start | bytes 393224 | tf_op jit(solution)/shard_map/ppermute | solution.py:398
  72.4 1.6 %collective-permute-start.14 = (f32[4,64,128]{2,1,0:T(8,128)}, f32[4,64,128]{2,1,0:T(8,128)S(1)}, u32[]{:S(2)}, u32[]{:S(2)}) collective-permute-start(f32[4,64,128]{2,1,0:T(8,128)} %get-tuple-element.13), channel_id=1, source_target_pairs={{0,3},{1,0},{2,1},{3,2},{4,7},{5,4},{6,5},{7,6},{8,11},{9,8},{10,9... | collective-permute-start | bytes 393224 | tf_op jit(solution)/shard_map/ppermute | solution.py:398
  75.4 6.5 %collective-permute-done.9 = f32[4,16,128]{2,1,0:T(8,128)S(1)} collective-permute-done((f32[4,16,128]{2,1,0:T(8,128)S(1)}, f32[4,16,128]{2,1,0:T(8,128)S(1)}, u32[]{:S(2)}, u32[]{:S(2)}) %collective-permute-start.9) | collective-permute-done | bytes 32800 | tf_op jit(solution)/shard_map/ppermute | solution.py:397
  81.9 3.4 %collective-permute-done.10 = f32[4,16,128]{2,1,0:T(8,128)S(1)} collective-permute-done((f32[4,16,128]{2,1,0:T(8,128)S(1)}, f32[4,16,128]{2,1,0:T(8,128)S(1)}, u32[]{:S(2)}, u32[]{:S(2)}) %collective-permute-start.10) | collective-permute-done | bytes 32800 | tf_op jit(solution)/shard_map/ppermute | solution.py:397
  87.4 12.7 %gather.1 = f32[2,128,128]{2,1,0:T(8,128)} custom-call(s32[128]{0:T(128)} %tile_ref.3, s32[128,128]{1,0:T(8,128)} %x_ref.3, s32[128,128]{1,0:T(8,128)} %y_ref.3, f32[2,128,128]{2,1,0:T(8,128)} %frac_ref.3, f32[128,128]{1,0:T(8,128)} %power_ref.3, f32[4,64,512]{2,1,0:T(8,128)} %copy-done), custom_call_target="tpu_custom_call" | custom-call | tf_op jit(solution)/shard_map/gather/pallas_call | solution.py:127
  (42 shorter events, 7.3 us)
Async XLA Ops:
  1.7 23.3 %collective-permute-start.6 = (f32[5,64,64]{2,1,0:T(8,128)S(1)}, f32[5,64,64]{2,1,0:T(8,128)S(1)}, u32[]{:S(2)}, u32[]{:S(2)}) collective-permute-start(f32[5,64,64]{2,1,0:T(8,128)S(1)} %get-tuple-element.22), channel_id=1, source_target_pairs={{1,0},{2,1},{3,2},{7,3},{6,7},{5,6},{4,5},{8,4},{9,8},{10,9},{11,1... | collective-permute-start | bytes 245768 | tf_op jit(solution)/shard_map/ppermute | solution.py:348
  3.6 21.3 %collective-permute-start.7 = (f32[5,64,64]{2,1,0:T(8,128)S(1)}, f32[5,64,64]{2,1,0:T(8,128)S(1)}, u32[]{:S(2)}, u32[]{:S(2)}) collective-permute-start(f32[5,64,64]{2,1,0:T(8,128)S(1)} %get-tuple-element.21), channel_id=1, source_target_pairs={{0,1},{1,2},{2,3},{3,7},{7,6},{6,5},{5,4},{4,8},{8,9},{9,10},{10,1... | collective-permute-start | bytes 245768 | tf_op jit(solution)/shard_map/ppermute | solution.py:349
  20.3 6.1 %collective-permute-start.2 = (f32[4,64,128]{2,1,0:T(8,128)S(1)}, f32[4,64,128]{2,1,0:T(8,128)S(1)}, u32[]{:S(2)}, u32[]{:S(2)}) collective-permute-start(f32[4,64,128]{2,1,0:T(8,128)S(1)} %get-tuple-element.17), channel_id=1, source_target_pairs={{0,3},{1,0},{2,1},{3,2},{4,7},{5,4},{6,5},{7,6},{8,11},{9,8},{10,9... | collective-permute-start | bytes 393224 | tf_op jit(solution)/shard_map/ppermute | solution.py:384
  22.4 12.3 %collective-permute-start.1 = (f32[4,64,128]{2,1,0:T(8,128)S(1)}, f32[4,64,128]{2,1,0:T(8,128)S(1)}, u32[]{:S(2)}, u32[]{:S(2)}) collective-permute-start(f32[4,64,128]{2,1,0:T(8,128)S(1)} %get-tuple-element.18), channel_id=1, source_target_pairs={{0,2},{1,3},{2,0},{3,1},{4,6},{5,7},{6,4},{7,5},{8,10},{9,11},{10,... | collective-permute-start | bytes 393224 | tf_op jit(solution)/shard_map/ppermute | solution.py:384
  23.4 11.4 %collective-permute-start = (f32[4,64,128]{2,1,0:T(8,128)S(1)}, f32[4,64,128]{2,1,0:T(8,128)S(1)}, u32[]{:S(2)}, u32[]{:S(2)}) collective-permute-start(f32[4,64,128]{2,1,0:T(8,128)S(1)} %get-tuple-element.16), channel_id=1, source_target_pairs={{0,1},{1,2},{2,3},{3,0},{4,5},{5,6},{6,7},{7,4},{8,9},{9,10},{10,1... | collective-permute-start | bytes 393224 | tf_op jit(solution)/shard_map/ppermute | solution.py:384
  25.1 19.7 %collective-permute-start.8 = (f32[5,48,256]{2,1,0:T(8,128)S(1)}, f32[5,48,256]{2,1,0:T(8,128)S(1)}, u32[]{:S(2)}, u32[]{:S(2)}) collective-permute-start(f32[5,48,256]{2,1,0:T(8,128)S(1)} %fusion.1), channel_id=1, source_target_pairs={{0,16},{16,0},{1,17},{17,1},{2,18},{18,2},{3,19},{19,3},{4,20},{20... | collective-permute-start | bytes 737288 | tf_op jit(solution)/shard_map/ppermute | solution.py:354
  35.8 7.0 %collective-permute-start.3 = (f32[4,64,64]{2,1,0:T(8,128)S(1)}, f32[4,64,64]{2,1,0:T(8,128)S(1)}, u32[]{:S(2)}, u32[]{:S(2)}) collective-permute-start(f32[4,64,64]{2,1,0:T(8,128)S(1)} %get-tuple-element.28), channel_id=1, source_target_pairs={{1,0},{2,1},{3,2},{7,3},{6,7},{5,6},{4,5},{8,4},{9,8},{10,9},{11,1... | collective-permute-start | bytes 196616 | tf_op jit(solution)/shard_map/ppermute | solution.py:348
  37.7 6.4 %collective-permute-start.4 = (f32[4,64,64]{2,1,0:T(8,128)S(1)}, f32[4,64,64]{2,1,0:T(8,128)S(1)}, u32[]{:S(2)}, u32[]{:S(2)}) collective-permute-start(f32[4,64,64]{2,1,0:T(8,128)S(1)} %get-tuple-element.27), channel_id=1, source_target_pairs={{0,1},{1,2},{2,3},{3,7},{7,6},{6,5},{5,4},{4,8},{8,9},{9,10},{10,1... | collective-permute-start | bytes 196616 | tf_op jit(solution)/shard_map/ppermute | solution.py:349
  44.2 6.8 %collective-permute-start.5 = (f32[4,48,256]{2,1,0:T(8,128)S(1)}, f32[4,48,256]{2,1,0:T(8,128)S(1)}, u32[]{:S(2)}, u32[]{:S(2)}) collective-permute-start(f32[4,48,256]{2,1,0:T(8,128)S(1)} %fusion.3), channel_id=1, source_target_pairs={{0,16},{16,0},{1,17},{17,1},{2,18},{18,2},{3,19},{19,3},{4,20},{20... | collective-permute-start | bytes 589832 | tf_op jit(solution)/shard_map/ppermute | solution.py:354
  68.5 5.5 %copy-start.2 = (f32[4,64,128]{2,1,0:T(8,128)S(1)}, f32[4,64,128]{2,1,0:T(8,128)}, u32[]{:S(2)}) copy-start(f32[4,64,128]{2,1,0:T(8,128)} %get-tuple-element.12) | copy-start | bytes 393220
  68.5 17.4 %collective-permute-start.12 = (f32[4,64,128]{2,1,0:T(8,128)}, f32[4,64,128]{2,1,0:T(8,128)S(1)}, u32[]{:S(2)}, u32[]{:S(2)}) collective-permute-start(f32[4,64,128]{2,1,0:T(8,128)} %get-tuple-element.13), channel_id=1, source_target_pairs={{0,1},{1,2},{2,3},{3,0},{4,5},{5,6},{6,7},{7,4},{8,9},{9,10},{10,1... | collective-permute-start | bytes 393224 | tf_op jit(solution)/shard_map/ppermute | solution.py:398
  70.2 16.4 %collective-permute-start.13 = (f32[4,64,128]{2,1,0:T(8,128)}, f32[4,64,128]{2,1,0:T(8,128)S(1)}, u32[]{:S(2)}, u32[]{:S(2)}) collective-permute-start(f32[4,64,128]{2,1,0:T(8,128)} %get-tuple-element.13), channel_id=1, source_target_pairs={{0,2},{1,3},{2,0},{3,1},{4,6},{5,7},{6,4},{7,5},{8,10},{9,11},{10,... | collective-permute-start | bytes 393224 | tf_op jit(solution)/shard_map/ppermute | solution.py:398
  72.4 14.2 %collective-permute-start.14 = (f32[4,64,128]{2,1,0:T(8,128)}, f32[4,64,128]{2,1,0:T(8,128)S(1)}, u32[]{:S(2)}, u32[]{:S(2)}) collective-permute-start(f32[4,64,128]{2,1,0:T(8,128)} %get-tuple-element.13), channel_id=1, source_target_pairs={{0,3},{1,0},{2,1},{3,2},{4,7},{5,4},{6,5},{7,6},{8,11},{9,8},{10,9... | collective-permute-start | bytes 393224 | tf_op jit(solution)/shard_map/ppermute | solution.py:398
  74.1 7.8 %collective-permute-start.9 = (f32[4,16,128]{2,1,0:T(8,128)S(1)}, f32[4,16,128]{2,1,0:T(8,128)S(1)}, u32[]{:S(2)}, u32[]{:S(2)}) collective-permute-start(f32[4,16,128]{2,1,0:T(8,128)S(1)} %get-tuple-element.25), channel_id=1, source_target_pairs={{0,1},{1,2},{2,3},{3,0},{4,5},{5,6},{6,7},{7,4},{8,9},{9,10},{10,1... | collective-permute-start | bytes 98312 | tf_op jit(solution)/shard_map/ppermute | solution.py:397
  74.5 0.9 copy-start.1
  74.5 10.8 %collective-permute-start.10 = (f32[4,16,128]{2,1,0:T(8,128)S(1)}, f32[4,16,128]{2,1,0:T(8,128)S(1)}, u32[]{:S(2)}, u32[]{:S(2)}) collective-permute-start(f32[4,16,128]{2,1,0:T(8,128)S(1)} %get-tuple-element.24), channel_id=1, source_target_pairs={{0,2},{1,3},{2,0},{3,1},{4,6},{5,7},{6,4},{7,5},{8,10},{9,11},{10,... | collective-permute-start | bytes 98312 | tf_op jit(solution)/shard_map/ppermute | solution.py:397
  81.9 4.1 %collective-permute-start.11 = (f32[4,16,128]{2,1,0:T(8,128)S(1)}, f32[4,16,128]{2,1,0:T(8,128)S(1)}, u32[]{:S(2)}, u32[]{:S(2)}) collective-permute-start(f32[4,16,128]{2,1,0:T(8,128)S(1)} %get-tuple-element.23), channel_id=1, source_target_pairs={{0,3},{1,0},{2,1},{3,2},{4,7},{5,4},{6,5},{7,6},{8,11},{9,8},{10,9... | collective-permute-start | bytes 98312 | tf_op jit(solution)/shard_map/ppermute | solution.py:397
  85.9 0.7 copy-start.3
  86.6 0.8 copy-start

commit v2 on v1

--- a/solution.py
+++ b/solution.py
@@ -7,18 +7,28 @@
 from jax.experimental.pallas import tpu as pltpu
 from jax.sharding import PartitionSpec as P
 
+
 BAND = 16
 HEAT_SWEEP_COUNT = 24
 LANES = 128
 SUB = 8
 HALO_X = 48
 HALO_Y = 64
+VMEM_GRANT = 16 * 1024 * 1024
 F32 = jnp.float32
 BF16 = jnp.bfloat16
 
 
 def iota(shape, dim):
     return lax.broadcasted_iota(jnp.int32, shape, dim)
+
+
+def near(value):
+    return pltpu.with_memory_space_constraint(value, pltpu.VMEM)
+
+
+def near_out(shape):
+    return pltpu.VMEM(shape, F32)
 
 
 def split2(value):
@@ -26,91 +36,125 @@
     return high, (value - high.astype(F32)).astype(BF16)
 
 
-def spread_kernel(tile_ref, x_ref, y_ref, frac_ref, power_ref, out_ref, acc_ref, *, unroll):
+def cell_rows(refs, b):
+    x_ref, y_ref, frac_ref, power_ref = refs
+    at = pl.ds(b, 1)
+    return x_ref[at, :], y_ref[at, :], frac_ref[0, at, :], frac_ref[1, at, :], power_ref[at, :]
+
+
+def onehot_of(column, shape, dim):
+    return (iota(shape, dim) == column).astype(F32).astype(BF16)
+
+
+def spread_kernel(tile_ref, base_ref, x_ref, y_ref, frac_ref, power_ref, *rest, unroll):
+    out_refs, acc_ref = rest[:-1], rest[-1]
     blocks, width = x_ref.shape
-    tiers, rows, columns = out_ref.shape
+    tiers, rows, span = out_refs[0].shape
     bands = rows // BAND
+    bases = [base_ref[n] for n in range(len(out_refs))]
     acc_ref[...] = jnp.zeros_like(acc_ref)
 
     def one(b):
-        x = x_ref[pl.ds(b, 1), :]
-        y = y_ref[pl.ds(b, 1), :]
-        fx = frac_ref[0, pl.ds(b, 1), :]
-        fy = frac_ref[1, pl.ds(b, 1), :]
-        p = power_ref[pl.ds(b, 1), :]
+        x, y, fx, fy, p = cell_rows((x_ref, y_ref, frac_ref, power_ref), b)
         band = iota((BAND, width), 0)
         flux = jnp.where(band == x, p * (1.0 - fx), jnp.where(band == x + 1, p * fx, 0.0))
-        low = split2(flux * (1.0 - fy))
-        high = split2(flux * fy)
-        weights = jnp.concatenate([low[0], low[1], high[0], high[1]], 0)
-        onehot = (iota((columns, width), 0) == y).astype(F32).astype(BF16)
-        maps = lax.dot_general(weights, onehot, (((1,), (1,)), ((), ())), preferred_element_type=F32)
-        return maps[0:BAND] + maps[BAND : 2 * BAND], maps[2 * BAND : 3 * BAND] + maps[3 * BAND :]
+        weights = []
+        for base in bases:
+            at = y - base
+            weights += split2(flux * jnp.where((at >= 0) & (at < span), 1.0 - fy, 0.0))
+            weights += split2(flux * jnp.where((at >= -1) & (at < span - 1), fy, 0.0))
+        onehot = onehot_of(lax.rem(y, span), (span, width), 0)
+        maps = lax.dot_general(
+            jnp.concatenate(weights, 0), onehot, (((1,), (1,)), ((), ())), preferred_element_type=F32
+        )
+        part = [maps[n * BAND : (n + 1) * BAND] for n in range(len(weights))]
+        return [part[n] + part[n + 1] for n in range(0, len(weights), 2)]
 
     def turn(g, carry):
-        for k in range(unroll):
-            b = g * unroll + k
-            low, high = one(b)
-            tile = tile_ref[b]
-            acc_ref[tile, 0] += low
-            acc_ref[tile, 1] += high
+        got = [one(g * unroll + k) for k in range(unroll)]
+        for k, maps in enumerate(got):
+            tile = tile_ref[g * unroll + k]
+            for n, value in enumerate(maps):
+                acc_ref[tile, n] += value
         return carry
 
     lax.fori_loop(0, blocks // unroll, turn, 0)
+    for n, out_ref in enumerate(out_refs):
+        for tile in range(tiers * bands):
+            band = tile % bands
+            out_ref[tile // bands, band * BAND : (band + 1) * BAND, :] = acc_ref[tile, 2 * n] + turned_lanes(
+                acc_ref[tile, 2 * n + 1], 1
+            )
+
+
+def turned_lanes(value, shift):
+    span = value.shape[1]
+    if span == LANES:
+        return pltpu.roll(value, shift % span, 1)
+    return jnp.concatenate([value[:, -shift % span :], value[:, : -shift % span]], 1)
+
+
+def spread(cells, bases, shape, unroll=8):
+    tiers, rows, span = shape
+    count = bases.shape[0]
+    tiles = tiers * (rows // BAND)
+    vmem = pl.BlockSpec(memory_space=pltpu.VMEM)
+    smem = pl.BlockSpec(memory_space=pltpu.SMEM)
+    return pl.pallas_call(
+        functools.partial(spread_kernel, unroll=unroll),
+        out_shape=(near_out(shape),) * count,
+        in_specs=[smem, smem] + [vmem] * 4,
+        out_specs=(vmem,) * count,
+        scratch_shapes=[pltpu.VMEM((tiles, 2 * count, BAND, span), F32)],
+        compiler_params=pltpu.CompilerParams(vmem_limit_bytes=VMEM_GRANT),
+        name="spread",
+    )(cells[0], bases, *cells[1:])
+
+
+def gather_kernel(tile_ref, base_ref, x_ref, y_ref, frac_ref, power_ref, *rest, count, rows, unroll):
+    adj_refs, (out_ref, maps_ref) = rest[:count], rest[-2:]
+    before_ref = rest[count] if len(rest) == count + 3 else None
+    blocks, width = x_ref.shape
+    tiers, _, span = adj_refs[0].shape
+    bands = rows // BAND
+    bases = [base_ref[n] for n in range(count)]
     for tile in range(tiers * bands):
         band = tile % bands
-        out_ref[tile // bands, band * BAND : (band + 1) * BAND, :] = acc_ref[tile, 0] + pltpu.roll(
-            acc_ref[tile, 1], 1, 1
-        )
-
-
-def spread(cell_x, cell_y, frac, power, block_tile, shape):
-    blocks, width = cell_x.shape
-    tiers, rows, columns = shape
-    tiles = tiers * (rows // BAND)
-    vmem = pl.BlockSpec(memory_space=pltpu.VMEM)
-    return pl.pallas_call(
-        functools.partial(spread_kernel, unroll=4),
-        out_shape=jax.ShapeDtypeStruct(shape, F32),
-        in_specs=[pl.BlockSpec(memory_space=pltpu.SMEM)] + [vmem] * 4,
-        out_specs=vmem,
-        scratch_shapes=[pltpu.VMEM((tiles, 2, BAND, columns), F32)],
-        name="spread",
-    )(block_tile, cell_x, cell_y, frac, power)
-
-
-def gather_kernel(tile_ref, x_ref, y_ref, frac_ref, power_ref, adj_ref, out_ref, maps_ref, *, unroll):
-    blocks, width = x_ref.shape
-    tiers, rows, columns = adj_ref.shape
-    bands = rows // BAND
-    for tile in range(tiers * bands):
-        band = tile % bands
-        field = adj_ref[tile // bands, band * BAND : (band + 1) * BAND, :]
-        along_x = pltpu.roll(field, BAND - 1, 0) - field
-        along_y = pltpu.roll(field, columns - 1, 1) - field
-        mixed = pltpu.roll(along_x, columns - 1, 1) - along_x
-        parts = split2(along_x) + split2(along_y) + split2(mixed)
-        for n, part in enumerate(parts):
-            maps_ref[tile, n * BAND : (n + 1) * BAND, :] = part
+        at = 0
+        for adj_ref in adj_refs:
+            field = adj_ref[tile // bands, band * BAND : (band + 1) * BAND, :]
+            for rest_of in (field, turned_lanes(field, -1)):
+                for _ in range(3):
+                    part = rest_of.astype(BF16)
+                    maps_ref[tile, at : at + BAND, :] = part
+                    rest_of = rest_of - part.astype(F32)
+                    at += BAND
 
     def one(b):
-        x = x_ref[pl.ds(b, 1), :]
-        y = y_ref[pl.ds(b, 1), :]
-        fx = frac_ref[0, pl.ds(b, 1), :]
-        fy = frac_ref[1, pl.ds(b, 1), :]
-        p = power_ref[pl.ds(b, 1), :]
-        onehot = (iota((columns, width), 0) == y).astype(F32).astype(BF16)
+        x, y, fx, fy, p = cell_rows((x_ref, y_ref, frac_ref, power_ref), b)
+        onehot = onehot_of(lax.rem(y, span), (span, width), 0)
         got = lax.dot_general(
             maps_ref[tile_ref[b]], onehot, (((1,), (0,)), ((), ())), preferred_element_type=F32
         )
-        along_x = got[0:BAND] + got[BAND : 2 * BAND]
-        along_y = got[2 * BAND : 3 * BAND] + got[3 * BAND : 4 * BAND]
-        mixed = got[4 * BAND : 5 * BAND] + got[5 * BAND : 6 * BAND]
-        here = iota((BAND, width), 0) == x
-        by_x = jnp.sum(jnp.where(here, along_x + fy * mixed, 0.0), 0, keepdims=True)
-        by_y = jnp.sum(jnp.where(here, along_y + fx * mixed, 0.0), 0, keepdims=True)
-        out_ref[0, pl.ds(b, 1), :] = p * by_x
-        out_ref[1, pl.ds(b, 1), :] = p * by_y
+        part = [got[n * BAND : (n + 1) * BAND] for n in range(6 * count)]
+        low = high = 0.0
+        for n, base in enumerate(bases):
+            at = y - base
+            mine = part[6 * n : 6 * n + 6]
+            low = jnp.where((at >= 0) & (at < span), mine[0] + (mine[1] + mine[2]), low)
+            high = jnp.where((at >= -1) & (at < span - 1), mine[3] + (mine[4] + mine[5]), high)
+        band = iota((BAND, width), 0)
+        here, beyond = band == x, band == x + 1
+        across = (1.0 - fy) * low + fy * high
+        along = high - low
+        by_x = jnp.where(beyond, across, jnp.where(here, -across, 0.0))
+        by_y = jnp.where(beyond, fx, jnp.where(here, 1.0 - fx, 0.0)) * along
+        rows_out = [p * jnp.sum(v, 0, keepdims=True) for v in (by_x, by_y)]
+        for k in range(2):
+            row = rows_out[k]
+            if before_ref is not None:
+                row = row + before_ref[k, pl.ds(b, 1), :]
+            out_ref[k, pl.ds(b, 1), :] = row
 
     def turn(g, carry):
         for k in range(unroll):
@@ -120,18 +164,22 @@
     lax.fori_loop(0, blocks // unroll, turn, 0)
 
 
-def gather(cell_x, cell_y, frac, power, block_tile, adjoint):
-    tiers, rows, columns = adjoint.shape
+def gather(cells, bases, adjoints, before, rows, unroll=8):
+    tiers, _, span = adjoints[0].shape
     tiles = tiers * (rows // BAND)
+    count = len(adjoints)
     vmem = pl.BlockSpec(memory_space=pltpu.VMEM)
+    smem = pl.BlockSpec(memory_space=pltpu.SMEM)
+    operands = [near(v) for v in adjoints] + ([] if before is None else [near(before)])
     return pl.pallas_call(
-        functools.partial(gather_kernel, unroll=4),
-        out_shape=jax.ShapeDtypeStruct(frac.shape, F32),
-        in_specs=[pl.BlockSpec(memory_space=pltpu.SMEM)] + [vmem] * 5,
+        functools.partial(gather_kernel, count=count, rows=rows, unroll=unroll),
+        out_shape=near_out(cells[3].shape),
+        in_specs=[smem, smem] + [vmem] * (4 + len(operands)),
         out_specs=vmem,
-        scratch_shapes=[pltpu.VMEM((tiles, 6 * BAND, columns), BF16)],
+        scratch_shapes=[pltpu.VMEM((tiles, 6 * BAND * count, span), BF16)],
+        compiler_params=pltpu.CompilerParams(vmem_limit_bytes=VMEM_GRANT),
         name="gather",
-    )(block_tile, cell_x, cell_y, frac, power, adjoint)
+    )(cells[0], bases, *cells[1:], *operands)
 
 
 def next_lane(pair, last):
@@ -233,17 +281,18 @@
     steps = cond_window.shape[2] // SUB
     shape = (tiers, 2, steps, SUB, LANES)
     vmem = pl.BlockSpec(memory_space=pltpu.VMEM)
-    sds = jax.ShapeDtypeStruct(shape, F32)
+    sds = near_out(shape)
     return pl.pallas_call(
         functools.partial(
             coef_kernel, tiers=tiers, rows=rows, span=span, grid_x=grid_x, grid_y=grid_y
         ),
-        out_shape=(sds, sds, jax.ShapeDtypeStruct((tiers - 1,) + shape[1:], F32), sds),
+        out_shape=(sds, sds, near_out((tiers - 1,) + shape[1:]), sds),
         in_specs=[pl.BlockSpec(memory_space=pltpu.SMEM), vmem],
         out_specs=(vmem,) * 4,
         scratch_shapes=[pltpu.VMEM(shape, F32)],
+        compiler_params=pltpu.CompilerParams(vmem_limit_bytes=VMEM_GRANT),
         name="coefs",
-    )(place, cond_window)
+    )(place, near(cond_window))
 
 
 def sweep(u_ref, q_ref, bx_ref, by_ref, bz_ref):
@@ -317,7 +366,7 @@
 def solve(p_window, bx, by, bz, scale, rows):
     tiers, _, steps = scale.shape[:3]
     vmem = pl.BlockSpec(memory_space=pltpu.VMEM)
-    sds = jax.ShapeDtypeStruct((tiers, rows, LANES), F32)
+    sds = near_out((tiers, rows, LANES))
     return pl.pallas_call(
         solve_kernel,
         out_shape=(sds, sds),
@@ -328,11 +377,12 @@
             pltpu.VMEM(scale.shape, F32),
             pltpu.VMEM((tiers, steps * SUB, LANES), F32),
         ],
+        compiler_params=pltpu.CompilerParams(vmem_limit_bytes=VMEM_GRANT),
         name="solve",
-    )(p_window, bx, by, bz, scale)
-
-
-def on_device(cell_x, cell_y, frac, power, block_tile, conductivity, sink):
+    )(*(near(v) for v in (p_window, bx, by, bz, scale)))
+
+
+def step(cell_x, cell_y, frac, power, block_tile, conductivity, sink):
     tiers, rows, columns = conductivity.shape
     n_sx, n_sy, n_net = (lax.axis_size(a) for a in ("sx", "sy", "net"))
     sx, sy, net = (lax.axis_index(a) for a in ("sx", "sy", "net"))
@@ -344,11 +394,7 @@
     to_right = list(zip(order[:-1], order[1:]))
     to_left = [(b, a) for a, b in to_right]
 
-    def window(chunk):
-        right = lax.ppermute(chunk[..., :HALO_Y], ("sy", "net"), to_left)
-        left = lax.ppermute(chunk[..., span - HALO_Y :], ("sy", "net"), to_right)
-        gap = jnp.zeros(chunk.shape[:-1] + (2 * LANES - span - 2 * HALO_Y,), F32)
-        strip = jnp.concatenate([chunk, right, gap, left], -1)
+    def with_rows(strip):
         if n_sx == 2:
             edge = lax.dynamic_slice_in_dim(strip, (1 - sx) * (rows - HALO_X), HALO_X, 1)
             parts = [strip, lax.ppermute(edge, "sx", [(0, 1), (1, 0)])]
@@ -358,11 +404,52 @@
             after = lax.ppermute(strip[:, :HALO_X], "sx", down)
             before = lax.ppermute(strip[:, rows - HALO_X :], "sx", up)
             parts = [strip, after, before]
-        full = jnp.concatenate(parts, 1)
+        return jnp.concatenate(parts, 1)
+
+    def window(chunk):
+        own = with_rows(chunk)
+        right = lax.ppermute(chunk[..., :HALO_Y], ("sy", "net"), to_left)
+        left = lax.ppermute(chunk[..., span - HALO_Y :], ("sy", "net"), to_right)
+        side = with_rows(jnp.concatenate([right, left], -1))
+        if span == LANES and 2 * HALO_Y == LANES:
+            return jnp.stack([own, side], 1)
+        gap = jnp.zeros(own.shape[:-1] + (2 * LANES - span - 2 * HALO_Y,), F32)
+        full = jnp.concatenate([own, side[..., :HALO_Y], gap, side[..., HALO_Y:]], -1)
         return jnp.stack([full[..., :LANES], full[..., LANES:]], 1)
 
+    paired = n_net & (n_net - 1) == 0
+
+    def partner(distance):
+        return net ^ distance if paired else (net + distance) % n_net
+
+    def source_of(distance):
+        return net ^ distance if paired else (net - distance) % n_net
+
+    def swap(value, distance):
+        ends = [(i, i ^ distance if paired else (i + distance) % n_net) for i in range(n_net)]
+        return lax.ppermute(value, "net", ends)
+
+    def base_of(rank):
+        return jnp.where(turned, n_net - 1 - rank, rank) * span
+
+    cells = (block_tile,) + tuple(near(v) for v in (cell_x, cell_y, frac, power))
+
+    def bases_of(distances, ranks):
+        return jnp.stack([base_of(ranks(d)) for d in distances]).astype(jnp.int32)
+
+    half = n_net // 2
+    far, close = list(range(n_net - 1, half - 1, -1)), list(range(half - 1, -1, -1))
+    shape = (tiers, rows, span)
+    made = spread(cells, bases_of(far, partner), shape, 32)
+    moved = [swap(value, d) for value, d in zip(made, far)]
+    close_bases, _ = lax.optimization_barrier((bases_of(close, partner), made[0]))
+    made = spread(cells, close_bases, shape, 32)
+    own = made[-1]
+    moved = [swap(value, d) for value, d in zip(made[:-1], close)] + moved
+
     material = jnp.concatenate([conductivity, sink[None]], 0)
-    cond_window = window(lax.dynamic_slice_in_dim(material, chunk_id * span, span, 2))
+    cond_chunk = lax.dynamic_slice_in_dim(material, chunk_id * span, span, 2)
+    cond_window = window(cond_chunk)
     total_rows = cond_window.shape[2]
     wrap = jnp.where(sx == 0, total_rows, rows) if n_sx == 2 else rows + HALO_X
     place = jnp.stack([sx * rows, wrap, (sy * n_net + chunk_id) * span]).astype(jnp.int32)
@@ -370,40 +457,34 @@
         place, cond_window, tiers, rows, span, n_sx * rows, n_sy * columns
     )
 
-    partial_map = spread(cell_x, cell_y, frac, power, block_tile, conductivity.shape)
-
-    def chunk_of(value, rank):
-        place_of = jnp.where(turned, n_net - 1 - rank, rank)
-        return lax.dynamic_slice_in_dim(value, place_of * span, span, 2)
-
-    def ring(distance):
-        return [(i, (i + distance) % n_net) for i in range(n_net)]
-
-    own = chunk_of(partial_map, net)
-    for d in range(1, n_net):
-        own = own + lax.ppermute(chunk_of(partial_map, (net + d) % n_net), "net", ring(d))
+    for value in moved:
+        own = own + value
     temp, adj = solve(window(own), bx, by, bz, scale, rows)
     temp, adj = temp[..., :span], adj[..., :span]
 
     share = rows // n_net
+
+    def state_rows(rank):
+        return lax.dynamic_slice_in_dim(temp, rank * share, share, 1)
+
+    pieces = {0: adj}
+    for d in range(n_net - 1, 0, -1):
+        pieces[d] = swap(jnp.concatenate([adj, state_rows(partner(d))], 1), d)
     temp_full = jnp.zeros((tiers, share, columns), F32)
-    adj_full = jnp.zeros((tiers, rows, columns), F32)
     for d in range(n_net):
-        source = (net - d) % n_net
-        at = jnp.where(turned, n_net - 1 - source, source) * span
-        piece = lax.dynamic_slice_in_dim(temp, (net + d) % n_net * share, share, 1)
-        adj_piece = adj
-        if d:
-            piece = lax.ppermute(piece, "net", ring(d))
-            adj_piece = lax.ppermute(adj, "net", ring(d))
-        temp_full = lax.dynamic_update_slice_in_dim(temp_full, piece, at, 2)
-        adj_full = lax.dynamic_update_slice_in_dim(adj_full, adj_piece, at, 2)
-    return temp_full, gather(cell_x, cell_y, frac, power, block_tile, adj_full)
+        piece = pieces[d][:, rows:] if d else state_rows(net)
+        temp_full = lax.dynamic_update_slice_in_dim(temp_full, piece, base_of(source_of(d)), 2)
+    grads = None
+    for group in (range(2), range(2, n_net)):
+        grads = gather(
+            cells, bases_of(group, source_of), [pieces[d] for d in group], grads, rows, 32
+        )
+    return temp_full, grads
 
 
 def solution(mesh):
     return jax.shard_map(
-        on_device,
+        step,
         mesh=mesh,
         in_specs=(
             P(("sx", "sy", "net"), None),

time: 102 us -> 79.8 us (0.78)
  the two profiles are of different devices: /device:TPU:6 before, /device:TPU:0 now
where the time goes in v2:
time: 79.8 us; the launch traced here: 79.6 us
  Pallas kernels  31.9 us (40%)
  starting transfers between devices  25.8 us (32%)
  waiting for transfers between devices  16.7 us (21%)
  local copies, waits for them, and re-layouts  2.17 us (3%)
  other arithmetic  2.02 us (3%)
  between operations  0.95 us (1%)
    pallas_call x1, Pallas kernels, solve(): pl.pallas_call(solve_kernel, out_shape=(sds, sds), in_specs=[vmem] * 5, o...  14.7 us
    ppermute x6, waiting for transfers between devices, swap(): return lax.ppermute(value, 'net', ends)  12.2 us
    ppermute x2, starting transfers between devices, window(): left = lax.ppermute(chunk[..., span - HALO_Y:], ('sy', 'net'), to_right)  10.1 us
    ppermute x6, starting transfers between devices, swap(): return lax.ppermute(value, 'net', ends)  9.5 us
    pallas_call x2, Pallas kernels, spread(): pl.pallas_call(functools.partial(spread_kernel, unroll=unroll), out_shape...  8.26 us
    pallas_call x2, Pallas kernels, gather(): pl.pallas_call(functools.partial(gather_kernel, count=count, rows=rows, u...  7.72 us
    ppermute x4, starting transfers between devices, with_rows(): parts = [strip, lax.ppermute(edge, 'sx', [(0, 1), (1, 0)])]  3.41 us
    ppermute x2, starting transfers between devices, window(): right = lax.ppermute(chunk[..., :HALO_Y], ('sy', 'net'), to_left)  2.72 us
  transfers between devices with their start and end apart: 14, of which 8 were waited for; matrix products, arithmetic and copies ran while one was open for 1% of the time, Pallas kernels for 17%

profile of v2, /device:TPU:0, one launch (start us, length us, event | category | flops | bytes accessed | tf_op | source)
XLA Modules:
  0.0 79.6 jit_solution(1507439545093106140)
XLA Ops:
  0.6 0.9 %fusion = f32[5,64,128]{2,1,0:T(8,128)S(1)} fusion(s32[]{:T(128)S(6)} %select_n.74, f32[4,64,512]{2,1,0:T(8,128)} %param.12, f32[1,64,512]{2,1,0:T(8,128)} %bitcast.20), kind=kLoop, calls=%fused_computation.13 | loop fusion | flops 40960 | bytes 819204 | tf_op jit(solution)/shard_map/concatenate | solution.py:450
  1.7 1.4 %collective-permute-start.8 = (f32[5,64,64]{2,1,0:T(8,128)S(1)}, f32[5,64,64]{2,1,0:T(8,128)S(1)}, u32[]{:S(2)}, u32[]{:S(2)}) collective-permute-start(f32[5,64,64]{2,1,0:T(8,128)S(1)} %get-tuple-element.25), channel_id=1, source_target_pairs={{1,0},{2,1},{3,2},{7,3},{6,7},{5,6},{4,5},{8,4},{9,8},{10,9},{11,1... | collective-permute-start | bytes 245768 | tf_op jit(solution)/shard_map/ppermute | solution.py:411
  3.1 5.6 %collective-permute-start.9 = (f32[5,64,64]{2,1,0:T(8,128)S(1)}, f32[5,64,64]{2,1,0:T(8,128)S(1)}, u32[]{:S(2)}, u32[]{:S(2)}) collective-permute-start(f32[5,64,64]{2,1,0:T(8,128)S(1)} %get-tuple-element.24), channel_id=1, source_target_pairs={{0,1},{1,2},{2,3},{3,7},{7,6},{6,5},{5,4},{4,8},{8,9},{9,10},{10,1... | collective-permute-start | bytes 245768 | tf_op jit(solution)/shard_map/ppermute | solution.py:412
  9.0 2.0 %collective-permute-start.7 = (f32[5,48,128]{2,1,0:T(8,128)S(1)}, f32[5,48,128]{2,1,0:T(8,128)S(1)}, u32[]{:S(2)}, u32[]{:S(2)}) collective-permute-start(f32[5,48,128]{2,1,0:T(8,128)S(1)} %fusion.2), channel_id=1, source_target_pairs={{0,16},{16,0},{1,17},{17,1},{2,18},{18,2},{3,19},{19,3},{4,20},{20... | collective-permute-start | bytes 368648 | tf_op jit(solution)/shard_map/ppermute | solution.py:400
  11.6 4.1 %spread.2 = (f32[4,64,128]{2,1,0:T(8,128)S(1)}, f32[4,64,128]{2,1,0:T(8,128)S(1)}) custom-call(s32[128]{0:T(128)S(1)} %copy-done.4, s32[2]{0:T(128)S(1)} %pad_add_fusion.1.base_ref, s32[128,128]{1,0:T(8,128)S(1)} %copy-done.1, s32[128,128]{1,0:T(8,128)S(1)} %copy-done.2, f32[2,128,128]{2,1,0:T(8,128)S(1)} %copy-done, f32[128,128]{1,0:T(8,128)S(1)} %copy-done.3), custom_call_target="tpu_custom_call" | custom-call | tf_op jit(solution)/shard_map/spread/pallas_call | solution.py:103
  15.8 2.1 %collective-permute-start.1 = (f32[4,64,128]{2,1,0:T(8,128)S(1)}, f32[4,64,128]{2,1,0:T(8,128)S(1)}, u32[]{:S(2)}, u32[]{:S(2)}) collective-permute-start(f32[4,64,128]{2,1,0:T(8,128)S(1)} %get-tuple-element.13), channel_id=1, source_target_pairs={{0,3},{1,2},{2,1},{3,0},{4,7},{5,6},{6,5},{7,4},{8,11},{9,10},{10,... | collective-permute-start | bytes 393224 | tf_op jit(solution)/shard_map/ppermute | solution.py:430
  18.0 4.1 %spread.3 = (f32[4,64,128]{2,1,0:T(8,128)S(1)}, f32[4,64,128]{2,1,0:T(8,128)S(1)}) custom-call(s32[128]{0:T(128)S(1)} %copy-done.4, s32[2]{0:T(128)S(1)} %pad_add_fusion.base_ref, s32[128,128]{1,0:T(8,128)S(1)} %copy-done.1, s32[128,128]{1,0:T(8,128)S(1)} %copy-done.2, f32[2,128,128]{2,1,0:T(8,128)S(1)} %copy-done, f32[128,128]{1,0:T(8,128)S(1)} %copy-done.3), custom_call_target="tpu_custom_call" | custom-call | tf_op jit(solution)/shard_map/spread/pallas_call | solution.py:103
  22.1 1.1 %collective-permute-start = (f32[4,64,128]{2,1,0:T(8,128)S(1)}, f32[4,64,128]{2,1,0:T(8,128)S(1)}, u32[]{:S(2)}, u32[]{:S(2)}) collective-permute-start(f32[4,64,128]{2,1,0:T(8,128)S(1)} %get-tuple-element.16), channel_id=1, source_target_pairs={{0,1},{1,0},{2,3},{3,2},{4,5},{5,4},{6,7},{7,6},{8,9},{9,8},{10,11... | collective-permute-start | bytes 393224 | tf_op jit(solution)/shard_map/ppermute | solution.py:430
  23.4 1.3 %collective-permute-start.2 = (f32[4,64,128]{2,1,0:T(8,128)S(1)}, f32[4,64,128]{2,1,0:T(8,128)S(1)}, u32[]{:S(2)}, u32[]{:S(2)}) collective-permute-start(f32[4,64,128]{2,1,0:T(8,128)S(1)} %get-tuple-element.17), channel_id=1, source_target_pairs={{0,2},{1,3},{2,0},{3,1},{4,6},{5,7},{6,4},{7,5},{8,10},{9,11},{10,... | collective-permute-start | bytes 393224 | tf_op jit(solution)/shard_map/ppermute | solution.py:430
  24.9 4.4 %collective-permute-done = f32[4,64,128]{2,1,0:T(8,128)S(1)} collective-permute-done((f32[4,64,128]{2,1,0:T(8,128)S(1)}, f32[4,64,128]{2,1,0:T(8,128)S(1)}, u32[]{:S(2)}, u32[]{:S(2)}) %collective-permute-start) | collective-permute-done | bytes 131104 | tf_op jit(solution)/shard_map/ppermute | solution.py:430
  29.4 2.4 %collective-permute-done.2 = f32[4,64,128]{2,1,0:T(8,128)S(1)} collective-permute-done((f32[4,64,128]{2,1,0:T(8,128)S(1)}, f32[4,64,128]{2,1,0:T(8,128)S(1)}, u32[]{:S(2)}, u32[]{:S(2)}) %collective-permute-start.2) | collective-permute-done | bytes 131104 | tf_op jit(solution)/shard_map/ppermute | solution.py:430
  31.9 1.3 %collective-permute-start.4 = (f32[4,64,64]{2,1,0:T(8,128)S(1)}, f32[4,64,64]{2,1,0:T(8,128)S(1)}, u32[]{:S(2)}, u32[]{:S(2)}) collective-permute-start(f32[4,64,64]{2,1,0:T(8,128)S(1)} %get-tuple-element.34), channel_id=1, source_target_pairs={{1,0},{2,1},{3,2},{7,3},{6,7},{5,6},{4,5},{8,4},{9,8},{10,9},{11,1... | collective-permute-start | bytes 196616 | tf_op jit(solution)/shard_map/ppermute | solution.py:411
  33.2 4.6 %collective-permute-start.5 = (f32[4,64,64]{2,1,0:T(8,128)S(1)}, f32[4,64,64]{2,1,0:T(8,128)S(1)}, u32[]{:S(2)}, u32[]{:S(2)}) collective-permute-start(f32[4,64,64]{2,1,0:T(8,128)S(1)} %get-tuple-element.33), channel_id=1, source_target_pairs={{0,1},{1,2},{2,3},{3,7},{7,6},{6,5},{5,4},{4,8},{8,9},{9,10},{10,1... | collective-permute-start | bytes 196616 | tf_op jit(solution)/shard_map/ppermute | solution.py:412
  38.4 1.1 %collective-permute-done.4 = f32[4,64,64]{2,1,0:T(8,128)S(1)} collective-permute-done((f32[4,64,64]{2,1,0:T(8,128)S(1)}, f32[4,64,64]{2,1,0:T(8,128)S(1)}, u32[]{:S(2)}, u32[]{:S(2)}) %collective-permute-start.4) | collective-permute-done | bytes 65568 | tf_op jit(solution)/shard_map/ppermute | solution.py:411
  39.5 0.8 collective-permute-done.5
  41.1 1.2 %coefs.1 = (f32[4,2,14,8,128]{4,3,2,1,0:T(8,128)S(1)}, f32[4,2,14,8,128]{4,3,2,1,0:T(8,128)S(1)}, f32[3,2,14,8,128]{4,3,2,1,0:T(8,128)S(1)}, f32[4,2,14,8,128]{4,3,2,1,0:T(8,128)S(1)}) custom-call(s32[3]{0:T(128)S(1)} %pad_add_fusion.2.place_ref, f32[5,2,112,128]{3,2,1,0:T(8,128)S(1)} %pad_maximum_fusion.cond_ref), custom_call_target="tpu_custom_call" | custom-call | tf_op jit(solution)/shard_map/coefs/pallas_call | solution.py:285
  42.9 2.1 %collective-permute-done.6 = f32[4,48,128]{2,1,0:T(8,128)S(1)} collective-permute-done((f32[4,48,128]{2,1,0:T(8,128)S(1)}, f32[4,48,128]{2,1,0:T(8,128)S(1)}, u32[]{:S(2)}, u32[]{:S(2)}) %collective-permute-start.6) | collective-permute-done | bytes 98336 | tf_op jit(solution)/shard_map/ppermute | solution.py:400
  45.2 14.7 %solve.1 = (f32[4,64,128]{2,1,0:T(8,128)S(1)}, f32[4,64,128]{2,1,0:T(8,128)S(1)}) custom-call(f32[4,2,112,128]{3,2,1,0:T(8,128)S(1)} %pad_maximum_fusion.1.p_ref, f32[4,2,14,8,128]{4,3,2,1,0:T(8,128)S(1)} %get-tuple-element.18.bx_ref, f32[4,2,14,8,128]{4,3,2,1,0:T(8,128)S(1)} %get-tuple-element.19.by_ref, ...), custom_call_target="tpu_custom_call" | custom-call | tf_op jit(solution)/shard_map/solve/pallas_call | solution.py:370
  60.0 2.5 %collective-permute-start.11 = (f32[4,80,128]{2,1,0:T(8,128)S(1)}, f32[4,80,128]{2,1,0:T(8,128)S(1)}, u32[]{:S(2)}, u32[]{:S(2)}) collective-permute-start(f32[4,80,128]{2,1,0:T(8,128)S(1)} %get-tuple-element.28), channel_id=1, source_target_pairs={{0,1},{1,0},{2,3},{3,2},{4,5},{5,4},{6,7},{7,6},{8,9},{9,8},{10,11... | collective-permute-start | bytes 491528 | tf_op jit(solution)/shard_map/ppermute | solution.py:430
  62.6 2.4 %collective-permute-start.13 = (f32[4,80,128]{2,1,0:T(8,128)S(1)}, f32[4,80,128]{2,1,0:T(8,128)S(1)}, u32[]{:S(2)}, u32[]{:S(2)}) collective-permute-start(f32[4,80,128]{2,1,0:T(8,128)S(1)} %get-tuple-element.26), channel_id=1, source_target_pairs={{0,3},{1,2},{2,1},{3,0},{4,7},{5,6},{6,5},{7,4},{8,11},{9,10},{10,... | collective-permute-start | bytes 491528 | tf_op jit(solution)/shard_map/ppermute | solution.py:430
  65.1 3.4 %collective-permute-done.11.rest_1_ = f32[4,80,128]{2,1,0:T(8,128)S(1)} collective-permute-done((f32[4,80,128]{2,1,0:T(8,128)S(1)}, f32[4,80,128]{2,1,0:T(8,128)S(1)}, u32[]{:S(2)}, u32[]{:S(2)}) %collective-permute-start.11) | collective-permute-done | bytes 163872 | tf_op jit(solution)/shard_map/ppermute | solution.py:430
  68.5 3.8 %gather.2.rest_2_ = f32[2,128,128]{2,1,0:T(8,128)S(1)} custom-call(s32[128]{0:T(128)S(1)} %copy-done.4, s32[2]{0:T(128)S(1)} %pad_add_fusion.4.base_ref, s32[128,128]{1,0:T(8,128)S(1)} %copy-done.1, s32[128,128]{1,0:T(8,128)S(1)} %copy-done.2, f32[2,128,128]{2,1,0:T(8,128)S(1)} %copy-done, f32[128,128]{1,0:T(8,128)S(1)} %copy-done.3, ...), custom_call_target="tpu_custom_call" | custom-call | tf_op jit(solution)/shard_map/gather/pallas_call | solution.py:174
  72.3 2.0 %collective-permute-done.12.rest_0_ = f32[4,80,128]{2,1,0:T(8,128)S(1)} collective-permute-done((f32[4,80,128]{2,1,0:T(8,128)S(1)}, f32[4,80,128]{2,1,0:T(8,128)S(1)}, u32[]{:S(2)}, u32[]{:S(2)}) %collective-permute-start.12) | collective-permute-done | bytes 163872 | tf_op jit(solution)/shard_map/ppermute | solution.py:430
  74.3 3.9 %gather.3 = f32[2,128,128]{2,1,0:T(8,128)S(1)} custom-call(s32[128]{0:T(128)S(1)} %copy-done.4, s32[2]{0:T(128)S(1)} %pad_add_fusion.3.base_ref, s32[128,128]{1,0:T(8,128)S(1)} %copy-done.1, s32[128,128]{1,0:T(8,128)S(1)} %copy-done.2, f32[2,128,128]{2,1,0:T(8,128)S(1)} %copy-done, f32[128,128]{1,0:T(8,128)S(1)} %copy-done.3, ...), custom_call_target="tpu_custom_call" | custom-call | tf_op jit(solution)/shard_map/gather/pallas_call | solution.py:174
  (52 shorter events, 5.3 us)
Async XLA Ops:
  1.6 7.2 %copy-start.5 = (f32[4,64,512]{2,1,0:T(8,128)S(1)}, f32[4,64,512]{2,1,0:T(8,128)}, u32[]{:S(2)}) copy-start(f32[4,64,512]{2,1,0:T(8,128)} %param.12) | copy-start | bytes 1572868
  1.6 7.2 %copy-start.6 = (f32[64,512]{1,0:T(8,128)S(1)}, f32[64,512]{1,0:T(8,128)}, u32[]{:S(2)}) copy-start(f32[64,512]{1,0:T(8,128)} %param.13) | copy-start | bytes 393220
  1.7 21.6 %collective-permute-start.8 = (f32[5,64,64]{2,1,0:T(8,128)S(1)}, f32[5,64,64]{2,1,0:T(8,128)S(1)}, u32[]{:S(2)}, u32[]{:S(2)}) collective-permute-start(f32[5,64,64]{2,1,0:T(8,128)S(1)} %get-tuple-element.25), channel_id=1, source_target_pairs={{1,0},{2,1},{3,2},{7,3},{6,7},{5,6},{4,5},{8,4},{9,8},{10,9},{11,1... | collective-permute-start | bytes 245768 | tf_op jit(solution)/shard_map/ppermute | solution.py:411
  3.1 21.5 %collective-permute-start.9 = (f32[5,64,64]{2,1,0:T(8,128)S(1)}, f32[5,64,64]{2,1,0:T(8,128)S(1)}, u32[]{:S(2)}, u32[]{:S(2)}) collective-permute-start(f32[5,64,64]{2,1,0:T(8,128)S(1)} %get-tuple-element.24), channel_id=1, source_target_pairs={{0,1},{1,2},{2,3},{3,7},{7,6},{6,5},{5,4},{4,8},{8,9},{9,10},{10,1... | collective-permute-start | bytes 245768 | tf_op jit(solution)/shard_map/ppermute | solution.py:412
  8.8 2.3 %copy-start = (f32[2,128,128]{2,1,0:T(8,128)S(1)}, f32[2,128,128]{2,1,0:T(8,128)}, u32[]{:S(2)}) copy-start(f32[2,128,128]{2,1,0:T(8,128)} %frac_ref.7) | copy-start | bytes 393220
  8.8 2.3 %copy-start.1 = (s32[128,128]{1,0:T(8,128)S(1)}, s32[128,128]{1,0:T(8,128)}, u32[]{:S(2)}) copy-start(s32[128,128]{1,0:T(8,128)} %x_ref.7) | copy-start | bytes 196612
  8.8 2.3 %copy-start.2 = (s32[128,128]{1,0:T(8,128)S(1)}, s32[128,128]{1,0:T(8,128)}, u32[]{:S(2)}) copy-start(s32[128,128]{1,0:T(8,128)} %y_ref.7) | copy-start | bytes 196612
  8.8 2.3 %copy-start.3 = (f32[128,128]{1,0:T(8,128)S(1)}, f32[128,128]{1,0:T(8,128)}, u32[]{:S(2)}) copy-start(f32[128,128]{1,0:T(8,128)} %power_ref.7) | copy-start | bytes 196612
  9.0 15.9 %collective-permute-start.7 = (f32[5,48,128]{2,1,0:T(8,128)S(1)}, f32[5,48,128]{2,1,0:T(8,128)S(1)}, u32[]{:S(2)}, u32[]{:S(2)}) collective-permute-start(f32[5,48,128]{2,1,0:T(8,128)S(1)} %fusion.2), channel_id=1, source_target_pairs={{0,16},{16,0},{1,17},{17,1},{2,18},{18,2},{3,19},{19,3},{4,20},{20... | collective-permute-start | bytes 368648 | tf_op jit(solution)/shard_map/ppermute | solution.py:400
  11.0 0.7 copy-start.4
  15.8 13.6 %collective-permute-start.1 = (f32[4,64,128]{2,1,0:T(8,128)S(1)}, f32[4,64,128]{2,1,0:T(8,128)S(1)}, u32[]{:S(2)}, u32[]{:S(2)}) collective-permute-start(f32[4,64,128]{2,1,0:T(8,128)S(1)} %get-tuple-element.13), channel_id=1, source_target_pairs={{0,3},{1,2},{2,1},{3,0},{4,7},{5,6},{6,5},{7,4},{8,11},{9,10},{10,... | collective-permute-start | bytes 393224 | tf_op jit(solution)/shard_map/ppermute | solution.py:430
  22.1 7.2 %collective-permute-start = (f32[4,64,128]{2,1,0:T(8,128)S(1)}, f32[4,64,128]{2,1,0:T(8,128)S(1)}, u32[]{:S(2)}, u32[]{:S(2)}) collective-permute-start(f32[4,64,128]{2,1,0:T(8,128)S(1)} %get-tuple-element.16), channel_id=1, source_target_pairs={{0,1},{1,0},{2,3},{3,2},{4,5},{5,4},{6,7},{7,6},{8,9},{9,8},{10,11... | collective-permute-start | bytes 393224 | tf_op jit(solution)/shard_map/ppermute | solution.py:430
  23.4 8.4 %collective-permute-start.2 = (f32[4,64,128]{2,1,0:T(8,128)S(1)}, f32[4,64,128]{2,1,0:T(8,128)S(1)}, u32[]{:S(2)}, u32[]{:S(2)}) collective-permute-start(f32[4,64,128]{2,1,0:T(8,128)S(1)} %get-tuple-element.17), channel_id=1, source_target_pairs={{0,2},{1,3},{2,0},{3,1},{4,6},{5,7},{6,4},{7,5},{8,10},{9,11},{10,... | collective-permute-start | bytes 393224 | tf_op jit(solution)/shard_map/ppermute | solution.py:430
  24.7 16.2 %collective-permute-start.10 = (f32[5,48,128]{2,1,0:T(8,128)S(1)}, f32[5,48,128]{2,1,0:T(8,128)S(1)}, u32[]{:S(2)}, u32[]{:S(2)}) collective-permute-start(f32[5,48,128]{2,1,0:T(8,128)S(1)} %fusion.1), channel_id=1, source_target_pairs={{0,16},{16,0},{1,17},{17,1},{2,18},{18,2},{3,19},{19,3},{4,20},{20... | collective-permute-start | bytes 368648 | tf_op jit(solution)/shard_map/ppermute | solution.py:400
  31.9 7.6 %collective-permute-start.4 = (f32[4,64,64]{2,1,0:T(8,128)S(1)}, f32[4,64,64]{2,1,0:T(8,128)S(1)}, u32[]{:S(2)}, u32[]{:S(2)}) collective-permute-start(f32[4,64,64]{2,1,0:T(8,128)S(1)} %get-tuple-element.34), channel_id=1, source_target_pairs={{1,0},{2,1},{3,2},{7,3},{6,7},{5,6},{4,5},{8,4},{9,8},{10,9},{11,1... | collective-permute-start | bytes 196616 | tf_op jit(solution)/shard_map/ppermute | solution.py:411
  33.2 7.1 %collective-permute-start.5 = (f32[4,64,64]{2,1,0:T(8,128)S(1)}, f32[4,64,64]{2,1,0:T(8,128)S(1)}, u32[]{:S(2)}, u32[]{:S(2)}) collective-permute-start(f32[4,64,64]{2,1,0:T(8,128)S(1)} %get-tuple-element.33), channel_id=1, source_target_pairs={{0,1},{1,2},{2,3},{3,7},{7,6},{6,5},{5,4},{4,8},{8,9},{9,10},{10,1... | collective-permute-start | bytes 196616 | tf_op jit(solution)/shard_map/ppermute | solution.py:412
  37.8 5.1 %collective-permute-start.3 = (f32[4,48,128]{2,1,0:T(8,128)S(1)}, f32[4,48,128]{2,1,0:T(8,128)S(1)}, u32[]{:S(2)}, u32[]{:S(2)}) collective-permute-start(f32[4,48,128]{2,1,0:T(8,128)S(1)} %constant_dynamic-slice_fusion.3), channel_id=1, source_target_pairs={{0,16},{16,0},{1,17},{17,1},{2,18},{18,2},{3,19},{19,3},{4,20},{20... | collective-permute-start | bytes 294920 | tf_op jit(solution)/shard_map/ppermute | solution.py:400
  40.3 4.7 %collective-permute-start.6 = (f32[4,48,128]{2,1,0:T(8,128)S(1)}, f32[4,48,128]{2,1,0:T(8,128)S(1)}, u32[]{:S(2)}, u32[]{:S(2)}) collective-permute-start(f32[4,48,128]{2,1,0:T(8,128)S(1)} %fusion.3), channel_id=1, source_target_pairs={{0,16},{16,0},{1,17},{17,1},{2,18},{18,2},{3,19},{19,3},{4,20},{20... | collective-permute-start | bytes 294920 | tf_op jit(solution)/shard_map/ppermute | solution.py:400
  60.0 8.5 %collective-permute-start.11 = (f32[4,80,128]{2,1,0:T(8,128)S(1)}, f32[4,80,128]{2,1,0:T(8,128)S(1)}, u32[]{:S(2)}, u32[]{:S(2)}) collective-permute-start(f32[4,80,128]{2,1,0:T(8,128)S(1)} %get-tuple-element.28), channel_id=1, source_target_pairs={{0,1},{1,0},{2,3},{3,2},{4,5},{5,4},{6,7},{7,6},{8,9},{9,8},{10,11... | collective-permute-start | bytes 491528 | tf_op jit(solution)/shard_map/ppermute | solution.py:430
  62.5 11.8 %collective-permute-start.12 = (f32[4,80,128]{2,1,0:T(8,128)S(1)}, f32[4,80,128]{2,1,0:T(8,128)S(1)}, u32[]{:S(2)}, u32[]{:S(2)}) collective-permute-start(f32[4,80,128]{2,1,0:T(8,128)S(1)} %get-tuple-element.27), channel_id=1, source_target_pairs={{0,2},{1,3},{2,0},{3,1},{4,6},{5,7},{6,4},{7,5},{8,10},{9,11},{10,... | collective-permute-start | bytes 491528 | tf_op jit(solution)/shard_map/ppermute | solution.py:430
  62.6 11.7 %collective-permute-start.13 = (f32[4,80,128]{2,1,0:T(8,128)S(1)}, f32[4,80,128]{2,1,0:T(8,128)S(1)}, u32[]{:S(2)}, u32[]{:S(2)}) collective-permute-start(f32[4,80,128]{2,1,0:T(8,128)S(1)} %get-tuple-element.26), channel_id=1, source_target_pairs={{0,3},{1,2},{2,1},{3,0},{4,7},{5,6},{6,5},{7,4},{8,11},{9,10},{10,... | collective-permute-start | bytes 491528 | tf_op jit(solution)/shard_map/ppermute | solution.py:430
  78.9 0.7 copy-start.7
